TPU v7x, 32 devices: a whole 2x2x4 slice. The times are simulated.
32 devices in a mesh: dp: 2 (over x), ctx: 16 (over z, y, core).
Axes of the slice: x: 2, y: 2, z: 4, core: 2. Of those that a mesh axis runs over, the one named last changes fastest.
Arguments:
- inputs: bfloat16 [2, 2048, 1024], P('dp', 'ctx'), may hold values from -6 to 6
- cotangent: bfloat16 [2, 2048, 1024], P('dp', 'ctx'), may hold values from -6 to 6
- block_ids: int32 [2, 2048], P('dp', 'ctx'), may hold values from 0 to 15, never falling along the last dimension, each value on 1 to 256 neighbouring positions
- ln1_gain: bfloat16 [1024], P(('dp', 'ctx')), may hold values from 0.5 to 1.5
- ln1_bias: bfloat16 [1024], P(('dp', 'ctx')), may hold values from -3 to 3
- w_qkv: bfloat16 [1024, 3072], P(('dp', 'ctx')), may hold values from -0.1875 to 0.1875
- b_qkv: bfloat16 [2048], P(('dp', 'ctx')), may hold values from -3 to 3
- w_out: bfloat16 [1024, 1024], P(('dp', 'ctx')), may hold values from -1.5 to 1.5
- b_out: bfloat16 [1024], P(('dp', 'ctx')), may hold values from -3 to 3
- ln2_gain: bfloat16 [1024], P(('dp', 'ctx')), may hold values from 0.5 to 1.5
- ln2_bias: bfloat16 [1024], P(('dp', 'ctx')), may hold values from -3 to 3
- w_fc: bfloat16 [1024, 4096], P(('dp', 'ctx')), may hold values from -0.1875 to 0.1875
- b_fc: bfloat16 [4096], P(('dp', 'ctx')), may hold values from -3 to 3
- w_proj: bfloat16 [4096, 1024], P(('dp', 'ctx')), may hold values from -0.09375 to 0.09375
- b_proj: bfloat16 [1024], P(('dp', 'ctx')), may hold values from -3 to 3
Outputs:
- output: bfloat16 [2, 2048, 1024], P('dp', 'ctx')
- input_grad: bfloat16 [2, 2048, 1024], P('dp', 'ctx')
- ln1_gain_grad: float32 [1024], P(('dp', 'ctx'))
- ln1_bias_grad: float32 [1024], P(('dp', 'ctx'))
- w_qkv_grad: float32 [1024, 3072], P(('dp', 'ctx'))
- b_qkv_grad: float32 [2048], P(('dp', 'ctx'))
- w_out_grad: float32 [1024, 1024], P(('dp', 'ctx'))
- b_out_grad: float32 [1024], P(('dp', 'ctx'))
- ln2_gain_grad: float32 [1024], P(('dp', 'ctx'))
- ln2_bias_grad: float32 [1024], P(('dp', 'ctx'))
- w_fc_grad: float32 [1024, 4096], P(('dp', 'ctx'))
- b_fc_grad: float32 [4096], P(('dp', 'ctx'))
- w_proj_grad: float32 [4096, 1024], P(('dp', 'ctx'))
- b_proj_grad: float32 [1024], P(('dp', 'ctx'))
Inputs may be any that keep to these rules, and one draw needn't show every extreme that they name: `block_ids`: in each sequence the block numbers start at 0, never fall from one token to the next and rise in steps of one; each block has 1 to 256 tokens, and some block has exactly 256.
All inputs are finite; a program needn't handle non-finite values.
Results may differ from a plain program's by a relative error of at most 0.017.
Values may be sent and summed in bfloat16 or wider, within the bound.
A program may use at most 192 MiB of HBM per device.

v0:
```python
import math

import jax
import jax.numpy as jnp
from jax import lax
from jax.sharding import PartitionSpec as P

HEADS = 16


EPSILON = 1e-05


def norm_affine(rows, gain, shift):
    centred = rows - jnp.mean(rows, axis=-1, keepdims=True)
    spread = jnp.mean(centred * centred, axis=-1, keepdims=True)
    return centred * lax.rsqrt(spread + EPSILON) * gain + shift


def gelu_tanh(values):
    return jax.nn.gelu(values, approximate=True)


def exp_weights(queries, key_rows, key_marks, query_marks, score_scale):
    scores = (
        jnp.einsum("qhd,khd->hqk", queries, key_rows, preferred_element_type=jnp.float32)
        * score_scale
    )
    allowed = key_marks[None, None, :] <= query_marks[None, :, None]
    return jnp.where(allowed, jnp.exp(scores), 0.0)


def stack_blocks(kv_rows, id_rows, head_count):
    length = kv_rows.shape[0]
    block_span = min(1024, length)
    block_count = length // block_span
    head_size = kv_rows.shape[1] // (2 * head_count)
    stacked = kv_rows.reshape(block_count, block_span, 2 * head_count, head_size)
    return (stacked, id_rows.astype(jnp.float32).reshape(block_count, block_span))


def attend_forward(queries, stacked, key_marks, query_marks, score_scale):
    head_count = queries.shape[1]
    query_last = query_marks[-1]

    def advance(running, pieces):
        key_block, mark_block = pieces

        def compute(current):
            totals, summed = current
            weights = exp_weights(
                queries, key_block[:, :head_count], mark_block, query_marks, score_scale
            )
            totals = totals + jnp.sum(weights, axis=-1)
            summed = summed + jnp.einsum(
                "hqk,khd->qhd",
                weights.astype(jnp.bfloat16),
                key_block[:, head_count:],
                preferred_element_type=jnp.float32,
            )
            return (totals, summed)

        def skipped(current):
            return current

        return (lax.cond(mark_block[0] <= query_last, compute, skipped, running), None)

    initial = (
        jnp.zeros((head_count, queries.shape[0]), jnp.float32),
        jnp.zeros(queries.shape, jnp.float32),
    )
    (totals, summed), _ = lax.scan(advance, initial, (stacked, key_marks))
    return (totals, summed / jnp.transpose(totals)[:, :, None])


def attend_backward(queries, stacked, key_marks, query_marks, score_scale, scaled_grad, ratio):
    head_count = queries.shape[1]
    query_last = query_marks[-1]
    span = stacked.shape[1]

    def advance(query_grad, pieces):
        key_block, mark_block = pieces

        def compute(current):
            key_rows = key_block[:, :head_count]
            value_rows = key_block[:, head_count:]
            weights = exp_weights(queries, key_rows, mark_block, query_marks, score_scale)
            probe = jnp.einsum(
                "qhd,khd->hqk", scaled_grad, value_rows, preferred_element_type=jnp.float32
            )
            score_grad = (weights * (probe - ratio[:, :, None])).astype(jnp.bfloat16)
            updated = current + jnp.einsum(
                "hqk,khd->qhd", score_grad, key_rows, preferred_element_type=jnp.float32
            )
            key_grad = (
                jnp.einsum("hqk,qhd->khd", score_grad, queries, preferred_element_type=jnp.float32)
                * score_scale
            )
            value_grad = jnp.einsum(
                "hqk,qhd->khd",
                weights.astype(jnp.bfloat16),
                scaled_grad,
                preferred_element_type=jnp.float32,
            )
            return (updated, jnp.concatenate([key_grad, value_grad], axis=1))

        def skipped(current):
            return (current, jnp.zeros((span, 2 * head_count, queries.shape[2]), jnp.float32))

        return lax.cond(mark_block[0] <= query_last, compute, skipped, query_grad)

    query_grad, block_grads = lax.scan(
        advance, jnp.zeros(queries.shape, jnp.float32), (stacked, key_marks)
    )
    flat_grads = block_grads.reshape(block_grads.shape[0] * block_grads.shape[1], -1)
    return (query_grad * score_scale, flat_grads)


def local(
    inputs,
    cotangent,
    block_ids,
    ln1_gain,
    ln1_bias,
    w_qkv,
    b_qkv,
    w_out,
    b_out,
    ln2_gain,
    ln2_bias,
    w_fc,
    b_fc,
    w_proj,
    b_proj,
):
    shards = (
        ln1_gain,
        ln1_bias,
        w_qkv,
        b_qkv,
        w_out,
        b_out,
        ln2_gain,
        ln2_bias,
        w_fc,
        b_fc,
        w_proj,
        b_proj,
    )
    gathered = (
        lax.all_gather(shards[0], ("dp", "ctx"), axis=0, tiled=True),
        lax.all_gather(shards[1], ("dp", "ctx"), axis=0, tiled=True),
        lax.all_gather(shards[2], ("dp", "ctx"), axis=0, tiled=True),
        lax.all_gather(shards[3], ("dp", "ctx"), axis=0, tiled=True),
        lax.all_gather(shards[4], ("dp", "ctx"), axis=0, tiled=True),
        lax.all_gather(shards[5], ("dp", "ctx"), axis=0, tiled=True),
        lax.all_gather(shards[6], ("dp", "ctx"), axis=0, tiled=True),
        lax.all_gather(shards[7], ("dp", "ctx"), axis=0, tiled=True),
        lax.all_gather(shards[8], ("dp", "ctx"), axis=0, tiled=True),
        lax.all_gather(shards[9], ("dp", "ctx"), axis=0, tiled=True),
        lax.all_gather(shards[10], ("dp", "ctx"), axis=0, tiled=True),
        lax.all_gather(shards[11], ("dp", "ctx"), axis=0, tiled=True),
    )
    (
        gain_one,
        bias_one,
        qkv_mat,
        qkv_bias,
        out_mat,
        out_bias,
        gain_two,
        bias_two,
        fc_mat,
        fc_bias,
        proj_mat,
        proj_bias,
    ) = gathered
    model_width = qkv_mat.shape[0]
    head_count = HEADS
    head_size = model_width // head_count
    score_scale = 1.0 / math.sqrt(head_size)
    residual = inputs[0].astype(jnp.float32)
    token_count = residual.shape[0]
    first_normed, first_back = jax.vjp(
        norm_affine, residual, gain_one.astype(jnp.float32), bias_one.astype(jnp.float32)
    )
    first_low = first_normed.astype(jnp.bfloat16)
    bias_full = jnp.concatenate(
        [
            qkv_bias[:model_width].astype(jnp.float32),
            jnp.zeros((model_width,), jnp.float32),
            qkv_bias[model_width:].astype(jnp.float32),
        ]
    )
    projected = (
        jnp.dot(first_low, qkv_mat, preferred_element_type=jnp.float32) + bias_full
    ).astype(jnp.bfloat16)
    queries = projected[:, :model_width].reshape(token_count, head_count, head_size)
    key_value = projected[:, model_width:]
    query_marks = block_ids[0].astype(jnp.float32)
    mark_low = block_ids[0].astype(jnp.bfloat16)
    kv_rows, id_rows = (
        lax.all_gather(key_value, "ctx", axis=0, tiled=True),
        lax.all_gather(mark_low, "ctx", axis=0, tiled=True),
    )
    stacked, key_marks = stack_blocks(kv_rows, id_rows, head_count)
    totals, attended = attend_forward(queries, stacked, key_marks, query_marks, score_scale)
    attended_low = attended.reshape(token_count, model_width).astype(jnp.bfloat16)
    middle = (
        residual
        + jnp.dot(attended_low, out_mat, preferred_element_type=jnp.float32)
        + out_bias.astype(jnp.float32)
    )
    second_normed, second_back = jax.vjp(
        norm_affine, middle, gain_two.astype(jnp.float32), bias_two.astype(jnp.float32)
    )
    second_low = second_normed.astype(jnp.bfloat16)
    hidden = jnp.dot(second_low, fc_mat, preferred_element_type=jnp.float32) + fc_bias.astype(
        jnp.float32
    )
    active, active_back = jax.vjp(gelu_tanh, hidden)
    active_low = active.astype(jnp.bfloat16)
    output = (
        middle
        + jnp.dot(active_low, proj_mat, preferred_element_type=jnp.float32)
        + proj_bias.astype(jnp.float32)
    )
    back_qkv, back_out, back_fc, back_proj = (
        lax.all_gather(w_qkv, ("dp", "ctx"), axis=0, tiled=True),
        lax.all_gather(w_out, ("dp", "ctx"), axis=0, tiled=True),
        lax.all_gather(w_fc, ("dp", "ctx"), axis=0, tiled=True),
        lax.all_gather(w_proj, ("dp", "ctx"), axis=0, tiled=True),
    )
    grad_low = cotangent[0]
    grad_out = grad_low.astype(jnp.float32)
    proj_grad = jnp.einsum("tf,td->fd", active_low, grad_low, preferred_element_type=jnp.float32)
    proj_bias_grad = jnp.sum(grad_out, axis=0)
    active_grad = jnp.einsum("td,fd->tf", grad_low, back_proj, preferred_element_type=jnp.float32)
    hidden_low = active_back(active_grad)[0].astype(jnp.bfloat16)
    fc_grad = jnp.einsum("td,tf->df", second_low, hidden_low, preferred_element_type=jnp.float32)
    fc_bias_grad = jnp.sum(hidden_low.astype(jnp.float32), axis=0)
    second_grad = jnp.einsum("tf,df->td", hidden_low, back_fc, preferred_element_type=jnp.float32)
    middle_part, gain_two_grad, bias_two_grad = second_back(second_grad)
    middle_grad = middle_part + grad_out
    branch_low = middle_grad.astype(jnp.bfloat16)
    out_grad = jnp.einsum("td,te->de", attended_low, branch_low, preferred_element_type=jnp.float32)
    out_bias_grad = jnp.sum(branch_low.astype(jnp.float32), axis=0)
    attended_grad = jnp.einsum(
        "te,de->td", branch_low, back_out, preferred_element_type=jnp.float32
    ).reshape(token_count, head_count, head_size)
    ratio = jnp.transpose(jnp.sum(attended_grad * attended, axis=-1)) / totals
    scaled_grad = (attended_grad / jnp.transpose(totals)[:, :, None]).astype(jnp.bfloat16)
    query_grad, kv_grad = attend_backward(
        queries, stacked, key_marks, query_marks, score_scale, scaled_grad, ratio
    )
    kv_mine = lax.psum_scatter(kv_grad.astype(jnp.bfloat16), "ctx", scatter_dimension=0, tiled=True)
    query_low = query_grad.reshape(token_count, model_width).astype(jnp.bfloat16)
    mixed_grad = jnp.concatenate([query_low, kv_mine], axis=1)
    qkv_grad = jnp.einsum("td,te->de", first_low, mixed_grad, preferred_element_type=jnp.float32)
    qkv_bias_grad = jnp.concatenate(
        [
            jnp.sum(query_low.astype(jnp.float32), axis=0),
            jnp.sum(kv_mine[:, model_width:].astype(jnp.float32), axis=0),
        ]
    )
    first_grad = jnp.einsum("te,de->td", mixed_grad, back_qkv, preferred_element_type=jnp.float32)
    input_part, gain_one_grad, bias_one_grad = first_back(first_grad)
    input_grad = middle_grad + input_part
    owned = (
        lax.psum_scatter(gain_one_grad, ("dp", "ctx"), scatter_dimension=0, tiled=True),
        lax.psum_scatter(bias_one_grad, ("dp", "ctx"), scatter_dimension=0, tiled=True),
        lax.psum_scatter(qkv_grad, ("dp", "ctx"), scatter_dimension=0, tiled=True),
        lax.psum_scatter(qkv_bias_grad, ("dp", "ctx"), scatter_dimension=0, tiled=True),
        lax.psum_scatter(out_grad, ("dp", "ctx"), scatter_dimension=0, tiled=True),
        lax.psum_scatter(out_bias_grad, ("dp", "ctx"), scatter_dimension=0, tiled=True),
        lax.psum_scatter(gain_two_grad, ("dp", "ctx"), scatter_dimension=0, tiled=True),
        lax.psum_scatter(bias_two_grad, ("dp", "ctx"), scatter_dimension=0, tiled=True),
        lax.psum_scatter(fc_grad, ("dp", "ctx"), scatter_dimension=0, tiled=True),
        lax.psum_scatter(fc_bias_grad, ("dp", "ctx"), scatter_dimension=0, tiled=True),
        lax.psum_scatter(proj_grad, ("dp", "ctx"), scatter_dimension=0, tiled=True),
        lax.psum_scatter(proj_bias_grad, ("dp", "ctx"), scatter_dimension=0, tiled=True),
    )
    return (
        output.astype(jnp.bfloat16)[None],
        input_grad.astype(jnp.bfloat16)[None],
        owned[0],
        owned[1],
        owned[2],
        owned[3],
        owned[4],
        owned[5],
        owned[6],
        owned[7],
        owned[8],
        owned[9],
        owned[10],
        owned[11],
    )


def solution(mesh):
    placed = (
        P("dp", "ctx", None),
        P("dp", "ctx", None),
        P("dp", "ctx"),
        P(("dp", "ctx")),
        P(("dp", "ctx")),
        P(("dp", "ctx"), None),
        P(("dp", "ctx")),
        P(("dp", "ctx"), None),
        P(("dp", "ctx")),
        P(("dp", "ctx")),
        P(("dp", "ctx")),
        P(("dp", "ctx"), None),
        P(("dp", "ctx")),
        P(("dp", "ctx"), None),
        P(("dp", "ctx")),
    )
    return jax.shard_map(
        local,
        mesh=mesh,
        in_specs=placed,
        out_specs=(
            P("dp", "ctx", None),
            P("dp", "ctx", None),
            P(("dp", "ctx")),
            P(("dp", "ctx")),
            P(("dp", "ctx"), None),
            P(("dp", "ctx")),
            P(("dp", "ctx"), None),
            P(("dp", "ctx")),
            P(("dp", "ctx")),
            P(("dp", "ctx")),
            P(("dp", "ctx"), None),
            P(("dp", "ctx")),
            P(("dp", "ctx"), None),
            P(("dp", "ctx")),
        ),
        check_vma=False,
    )
```

profile of v0, /device:TPU:0, one launch (start us, length us, event | category | flops | bytes accessed | tf_op | source)
XLA Modules:
  0.0 1257.9 jit_solution(3312231048897050198)
XLA Ops:
  7.2 0.7 all-gather.8.cloned.1.call-update
  8.0 0.8 dynamic-update-slice.1
  8.8 0.8 dynamic-update-slice
  9.7 0.8 dynamic-update-slice.3
  10.5 0.8 dynamic-update-slice.6
  11.3 0.8 dynamic-update-slice.5
  12.2 0.8 dynamic-update-slice.4
  13.0 0.8 dynamic-update-slice.2
  13.8 42.5 %all-reduce.16 = (bf16[2048]{0:T(1024)(128)(2,1)S(1)}, bf16[1024]{0:T(1024)(128)(2,1)S(1)}, bf16[1024]{0:T(1024)(128)(2,1)S(1)}, bf16[1024]{0:T(1024)(128)(2,1)S...) all-reduce(bf16[2048]{0:T(1024)(128)(2,1)S(1)} %dynamic-update-slic, ...), channel_id=1, replica_groups=mesh['dp'=2,'ctx'=16] {'dp','ctx'}, use_global_device_ids=true, to_apply=%add.2 | all-reduce | flops 8192 | bytes 32768
  56.4 1.1 convert_reduce_fusion.2
  57.5 1.2 fusion.62
  58.7 24.6 %all-gather.8.cloned.1.call-done = bf16[1024,3072]{1,0:T(8,128)(2,1)} async-done(((bf16[32,3072]{1,0:T(8,128)(2,1)}), bf16[1024,3072]{1,0:T(8,128)(2,1)}) %all-gather.8.cloned.1.call-update) | async-done | bytes 6291472 | tf_op jit(solution)/shard_map/all_gather | solution.py:153
  83.4 4.0 fusion.40
  87.4 0.8 slice.54
  88.3 0.7 all-gather.12.cloned.1.call-update
  90.8 19.9 %all-gather = bf16[1,2048]{1,0:T(2,128)(2,1)S(1)} all-gather(bf16[1,128]{1,0:T(2,128)(2,1)S(1)} %get-tuple-element.334), channel_id=2, replica_groups=mesh['dp'=2,'ctx'=16] {'ctx'}, dimensions={1}, use_global_device_ids=true | all-gather | bytes 4352 | tf_op jit(solution)/shard_map/all_gather | solution.py:204
  111.3 36.6 %all-gather.1 = bf16[32,1,128]{2,1,0:T(2,128)(2,1)S(1)} all-gather(bf16[1,1,128]{2,1,0:T(2,128)(2,1)S(1)} %bitcast.154), channel_id=1, replica_groups=mesh['dp'=2,'ctx'=16] {'dp','ctx'}, dimensions={0}, use_global_device_ids=true | all-gather | bytes 8448 | tf_op jit(solution)/shard_map/all_gather | solution.py:160
  150.0 11.9 all-gather.10.cloned.1.call-done
  161.9 24.4 %reshape.233 = bf16[2,1024,32,64]{3,2,1,0:T(8,128)(2,1)} reshape(bf16[2048,2048]{1,0:T(8,128)(2,1)} %all-gather.10.cloned.1.call-done) | data formatting | bytes 16777216 | tf_op jit(solution)/shard_map/reshape | solution.py:38
  186.3 18.3 %copy.56 = bf16[2,1024,32,64]{1,3,2,0:T(8,128)(2,1)} copy(bf16[2,1024,32,64]{3,2,1,0:T(8,128)(2,1)} %reshape.233) | data formatting | bytes 16777216 | tf_op jit(solution)/shard_map/while | solution.py:72
  204.8 11.3 while.27
  206.6 7.4 conditional.4
  206.8 2.6 dynamic-slice_bitcast_fusion
  209.5 2.6 fusion.1
  212.1 1.9 fusion.13
  216.2 3.4 all-gather.12.cloned.1.call-done
  219.5 2.1 fusion.86
  221.9 76.8 %all-gather.14.cloned.1.call-done = bf16[1024,4096]{1,0:T(8,128)(2,1)} async-done(((bf16[32,4096]{1,0:T(8,128)(2,1)}), bf16[1024,4096]{1,0:T(8,128)(2,1)}) %all-gather.14.cloned.1.call-update) | async-done | bytes 8388624 | tf_op jit(solution)/shard_map/all_gather | solution.py:159
  298.8 4.7 convolution_add_fusion
  303.5 74.2 %all-gather.16.cloned.1.call-done = bf16[4096,1024]{1,0:T(8,128)(2,1)} async-done(((bf16[128,1024]{1,0:T(8,128)(2,1)}), bf16[4096,1024]{1,0:T(8,128)(2,1)}) %all-gather.16.cloned.1.call-update) | async-done | bytes 8388624 | tf_op jit(solution)/shard_map/all_gather | solution.py:161
  377.7 7.9 convert_reduce_fusion
  385.6 3.5 multiply_reduce_fusion
  389.4 0.8 convert_reduce_fusion.3
  390.2 0.7 fusion.88
  391.2 21.8 %while.28 = (s32[]{:T(128)}, f32[128,16,64]{0,2,1:T(8,128)S(1)}, bf16[2,1024,32,64]{1,3,2,0:T(8,128)(2,1)}, f32[2,1024]{1,0:T(2,128)S(1)}, f32[]{:T(128)}, /*ind...) while((s32[]{:T(128)}, f32[128,16,64]{0,2,1:T(8,128)S(1)}, ...), condition=%wide.region_15.16_spmd, body=%wide.region_12.15_spmd.sunk | while | flops 1363410944 | bytes 80106720 | solution.py:112
  393.2 12.0 conditional.5
  393.2 2.9 dynamic-slice_bitcast_fusion.1
  396.2 1.4 fusion.87
  397.7 3.0 fusion.20
  400.7 0.9 fusion.35
  401.6 1.7 fusion.27
  403.3 1.6 multiply_bitcast_fusion
  405.3 2.7 constant_dynamic-update-slice_fusion.2
  410.3 2.7 constant_dynamic-update-slice_fusion.2
  413.0 23.9 %copy.69 = bf16[2,1024,32,64]{3,2,1,0:T(8,128)(2,1)} copy(bf16[2,1024,32,64]{1,3,2,0:T(8,128)(2,1)} %get-tuple-element.206) | data formatting | bytes 16777216
  436.9 23.4 %reshape.231 = bf16[2048,2048]{1,0:T(8,128)(2,1)} reshape(bf16[2,1024,32,64]{3,2,1,0:T(8,128)(2,1)} %copy.69) | data formatting | bytes 16777216
  460.4 0.9 copy-done.17
  461.4 2.8 fusion.89
  464.8 110.5 %reduce-scatter.16.cloned.1.call-done = bf16[128,2048]{1,0:T(8,128)(2,1)} async-done(((bf16[2048,2048]{1,0:T(8,128)(2,1)}), bf16[128,2048]{1,0:T(8,128)(2,1)}) %reduce-scatter.16.cloned.1.call-update) | async-done | bytes 524304
  575.2 1.3 copy.66
  576.6 6.4 fusion.64
  583.1 0.9 copy-done.2
  584.5 8.2 fusion.82
  592.7 1.5 copy-done.6
  594.3 8.1 fusion.68
  602.4 0.6 copy-done.45
  603.1 5.7 fusion.51
  609.1 5.2 fusion.83
  614.7 41.8 %all-reduce.15 = (f32[1024]{0:T(1024)S(1)}, f32[1024]{0:T(1024)S(1)}, f32[2048]{0:T(1024)S(1)}, f32[1024]{0:T(1024)S(1)}, f32[1024]{0:T(1024)S(1)}, /*index=5*/f...) all-reduce(f32[1024]{0:T(1024)S(1)} %get-tuple-element.263, ...), channel_id=4, replica_groups=mesh['dp'=2,'ctx'=16] {'dp','ctx'}, use_global_device_ids=true, to_apply=%region_20.21.clone | all-reduce | flops 12288 | bytes 98304
  661.1 1.0 fusion.67
  662.1 57.4 %reduce-scatter.10.cloned.1.call-done = f32[32,1024]{1,0:T(8,128)} async-done(((f32[1024,1024]{1,0:T(8,128)}), f32[32,1024]{1,0:T(8,128)}) %reduce-scatter.10.cloned.1.call-update) | async-done | bytes 131088 | tf_op jit(solution)/shard_map/reduce_scatter | solution.py:274
  719.5 157.9 %reduce-scatter.8.cloned.1.call-done = f32[32,3072]{1,0:T(8,128)} async-done(((f32[1024,3072]{1,0:T(8,128)}), f32[32,3072]{1,0:T(8,128)}) %reduce-scatter.8.cloned.1.call-update) | async-done | bytes 393232 | tf_op jit(solution)/shard_map/reduce_scatter | solution.py:272
  877.4 185.8 %reduce-scatter.12.cloned.1.call-done = f32[32,4096]{1,0:T(8,128)} async-done(((f32[1024,4096]{1,0:T(8,128)}), f32[32,4096]{1,0:T(8,128)}) %reduce-scatter.12.cloned.1.call-update) | async-done | bytes 524304 | tf_op jit(solution)/shard_map/reduce_scatter | solution.py:278
  1063.2 187.4 %reduce-scatter.14.cloned.1.call-done = f32[128,1024]{1,0:T(8,128)} async-done(((f32[4096,1024]{1,0:T(8,128)}), f32[128,1024]{1,0:T(8,128)}) %reduce-scatter.14.cloned.1.call-update) | async-done | bytes 524304 | tf_op jit(solution)/shard_map/reduce_scatter | solution.py:280
  (182 shorter events, 15.9 us)
Async XLA Ops:
  7.2 76.2 %all-gather.8.cloned.1.call-start = ((), (), s32[]{:S(2)}) async-start(), calls=%async_computation.5 | async-start | bytes 6488064 | tf_op jit(solution)/shard_map/all_gather | solution.py:153
  7.9 154.0 %all-gather.10.cloned.1.call-start = ((), (), s32[]{:S(2)}) async-start(), calls=%async_computation.6 | async-start | bytes 8912896 | tf_op jit(solution)/shard_map/all_gather | solution.py:203
  56.4 31.0 %copy-start.24 = (f32[1024]{0:T(1024)}, f32[1024]{0:T(1024)S(1)}, u32[]{:S(2)}) copy-start(f32[1024]{0:T(1024)S(1)} %convert_element_type.133) | copy-start | bytes 12292
  56.4 31.0 %copy-start.20 = (f32[1024]{0:T(1024)}, f32[1024]{0:T(1024)S(1)}, u32[]{:S(2)}) copy-start(f32[1024]{0:T(1024)S(1)} %convert_element_type.132) | copy-start | bytes 12292
  57.5 29.9 %copy-start.29 = (f32[128]{0:T(128)}, f32[128]{0:T(128)S(1)}, u32[]{:S(2)}) copy-start(f32[128]{0:T(128)S(1)} %broadcast_multiply_fusion.1) | copy-start | bytes 1540
  58.7 28.7 %copy-start.46 = (f32[128]{0:T(128)}, f32[128]{0:T(128)S(1)}, u32[]{:S(2)}) copy-start(f32[128]{0:T(128)S(1)} %fusion.62) | copy-start | bytes 1540
  58.7 28.7 %copy-start.33 = (f32[128]{0:T(128)}, f32[128]{0:T(128)S(1)}, u32[]{:S(2)}) copy-start(f32[128]{0:T(128)S(1)} %fusion.75) | copy-start | bytes 1540
  58.7 32.1 %copy-start.49 = (s32[1,128]{1,0:T(1,128)S(1)}, s32[1,128]{1,0:T(1,128)}, u32[]{:S(2)}) copy-start(s32[1,128]{1,0:T(1,128)} %param.25) | copy-start | bytes 1540
  58.7 52.6 %copy-start.48 = (bf16[128]{0:T(256)(128)(2,1)S(1)}, bf16[128]{0:T(256)(128)(2,1)}, u32[]{:S(2)}) copy-start(bf16[128]{0:T(256)(128)(2,1)} %param.35) | copy-start | bytes 772
  88.3 131.3 %all-gather.12.cloned.1.call-start = ((), (), s32[]{:S(2)}) async-start(), calls=%async_computation.7 | async-start | bytes 2162688 | tf_op jit(solution)/shard_map/all_gather | solution.py:155
  89.0 209.8 %all-gather.14.cloned.1.call-start = ((), (), s32[]{:S(2)}) async-start(), calls=%async_computation.8 | async-start | bytes 8650752 | tf_op jit(solution)/shard_map/all_gather | solution.py:159
  89.6 288.1 %all-gather.16.cloned.1.call-start = ((), (), s32[]{:S(2)}) async-start(), calls=%async_computation.9 | async-start | bytes 8650752 | tf_op jit(solution)/shard_map/all_gather | solution.py:161
  90.2 485.1 %reduce-scatter.16.cloned.1.call-start = ((), (), s32[]{:S(2)}) async-start(), calls=%async_computation.14 | async-start | bytes 8912896
  204.7 14.8 %copy-start.3 = (bf16[1,128,1024]{2,1,0:T(8,128)(2,1)S(1)}, bf16[1,128,1024]{2,1,0:T(8,128)(2,1)}, u32[]{:S(2)}) copy-start(bf16[1,128,1024]{2,1,0:T(8,128)(2,1)} %param.23) | copy-start | bytes 786436
  204.8 14.8 %copy-start.41 = (f32[1024]{0:T(1024)S(1)}, f32[1024]{0:T(1024)}, u32[]{:S(2)}) copy-start(f32[1024]{0:T(1024)} %convert_element_type.140) | copy-start | bytes 12292
  216.1 82.7 %copy-start.22 = (f32[1024]{0:T(1024)S(1)}, f32[1024]{0:T(1024)}, u32[]{:S(2)}) copy-start(f32[1024]{0:T(1024)} %convert_element_type.141) | copy-start | bytes 12292
  216.1 82.7 %copy-start.26 = (f32[1024]{0:T(1024)S(1)}, f32[1024]{0:T(1024)}, u32[]{:S(2)}) copy-start(f32[1024]{0:T(1024)} %convert_element_type.142) | copy-start | bytes 12292
  216.1 82.7 %copy-start.28 = (f32[32,1,128]{2,1,0:T(1,128)S(1)}, f32[32,1,128]{2,1,0:T(1,128)}, u32[]{:S(2)}) copy-start(f32[32,1,128]{2,1,0:T(1,128)} %convert_element_type.161) | copy-start | bytes 49156
  216.2 82.6 %copy-start.16 = (bf16[128,16,64]{0,2,1:T(8,128)(2,1)}, bf16[128,16,64]{0,2,1:T(8,128)(2,1)S(1)}, u32[]{:S(2)}) copy-start(bf16[128,16,64]{0,2,1:T(8,128)(2,1)S(1)} %fusion.74) | copy-start | bytes 786436
  221.7 167.5 %copy-start.1 = (f32[128,1024]{1,0:T(8,128)}, f32[128,1024]{1,0:T(8,128)S(1)}, u32[]{:S(2)}) copy-start(f32[128,1024]{1,0:T(8,128)S(1)} %get-tuple-element.336) | copy-start | bytes 1572868
  221.7 167.4 %copy-start.31 = (f32[128]{0:T(128)}, f32[128]{0:T(128)S(1)}, u32[]{:S(2)}) copy-start(f32[128]{0:T(128)S(1)} %broadcast_multiply_fusion) | copy-start | bytes 1540
  221.9 167.2 %copy-start.35 = (f32[128]{0:T(128)}, f32[128]{0:T(128)S(1)}, u32[]{:S(2)}) copy-start(f32[128]{0:T(128)S(1)} %fusion.76) | copy-start | bytes 1540
  303.5 82.0 %copy-start.5 = (f32[128,4096]{1,0:T(8,128)}, f32[128,4096]{1,0:T(8,128)S(1)}, u32[]{:S(2)}) copy-start(f32[128,4096]{1,0:T(8,128)S(1)} %convolution_add_fusion) | copy-start | bytes 6291460
  377.7 7.9 copy-start
  385.5 3.6 copy-start.10
  385.5 3.9 copy-start.14
  385.5 4.7 copy-start.7
  389.4 1.7 copy-start.8
  389.4 0.8 copy-start.43
  390.2 0.9 copy-start.18
  460.4 0.9 copy-start.17
  460.4 1.0 copy-start.19
  460.4 259.1 %reduce-scatter.10.cloned.1.call-start = ((), (), s32[]{:S(2)}) async-start(), calls=%async_computation.11 | async-start | bytes 4325376 | tf_op jit(solution)/shard_map/reduce_scatter | solution.py:274
  464.2 112.4 %copy-start.4 = (bf16[1,128,1024]{2,1,0:T(8,128)(2,1)S(1)}, bf16[1,128,1024]{2,1,0:T(8,128)(2,1)}, u32[]{:S(2)}) copy-start(bf16[1,128,1024]{2,1,0:T(8,128)(2,1)} %param.23) | copy-start | bytes 786436
  464.2 112.4 %copy-start.21 = (f32[1024]{0:T(1024)S(1)}, f32[1024]{0:T(1024)}, u32[]{:S(2)}) copy-start(f32[1024]{0:T(1024)} %copy-done.20) | copy-start | bytes 12292
  464.2 112.4 %copy-start.25 = (f32[1024]{0:T(1024)S(1)}, f32[1024]{0:T(1024)}, u32[]{:S(2)}) copy-start(f32[1024]{0:T(1024)} %copy-done.24) | copy-start | bytes 12292
  464.2 112.4 %copy-start.30 = (f32[128]{0:T(128)S(1)}, f32[128]{0:T(128)}, u32[]{:S(2)}) copy-start(f32[128]{0:T(128)} %copy-done.29) | copy-start | bytes 1540
  464.2 112.4 %copy-start.34 = (f32[128]{0:T(128)S(1)}, f32[128]{0:T(128)}, u32[]{:S(2)}) copy-start(f32[128]{0:T(128)} %copy-done.33) | copy-start | bytes 1540
  464.2 413.2 %reduce-scatter.8.cloned.1.call-start = ((), (), s32[]{:S(2)}) async-start(), calls=%async_computation.10 | async-start | bytes 12976128 | tf_op jit(solution)/shard_map/reduce_scatter | solution.py:272
  576.5 6.5 copy-start.12
  583.0 1.1 copy-start.2
  583.0 1.4 copy-start.11
  583.0 1.4 copy-start.23
  583.0 1.4 copy-start.27
  583.0 1.4 copy-start.32
  583.0 1.4 copy-start.36
  583.1 480.2 %reduce-scatter.12.cloned.1.call-start = ((), (), s32[]{:S(2)}) async-start(), calls=%async_computation.12 | async-start | bytes 17301504 | tf_op jit(solution)/shard_map/reduce_scatter | solution.py:278
  592.6 1.6 copy-start.6
  592.7 1.6 copy-start.15
  592.7 658.0 %reduce-scatter.14.cloned.1.call-start = ((), (), s32[]{:S(2)}) async-start(), calls=%async_computation.13 | async-start | bytes 17301504 | tf_op jit(solution)/shard_map/reduce_scatter | solution.py:280
  602.4 0.7 copy-start.45
  603.1 5.7 copy-start.13
  608.8 5.4 copy-start.47
  609.0 5.6 copy-start.37
  609.0 5.6 copy-start.38
  609.0 5.6 copy-start.39
  609.0 5.6 copy-start.40
  609.0 5.6 copy-start.42
  609.0 52.0 %copy-start.9 = (f32[128,1024]{1,0:T(8,128)S(1)}, f32[128,1024]{1,0:T(8,128)}, u32[]{:S(2)}) copy-start(f32[128,1024]{1,0:T(8,128)} %copy-done.8) | copy-start | bytes 1572868
  609.1 52.0 %copy-start.44 = (f32[128]{0:T(128)S(1)}, f32[128]{0:T(128)}, u32[]{:S(2)}) copy-start(f32[128]{0:T(128)} %copy-done.43) | copy-start | bytes 1540
Sparse Core Ops, SparseCore 0:
  10.9 72.4 all-gather.7
  88.4 73.4 all-gather.9
  164.8 54.6 all-gather.11
  222.2 76.4 all-gather.13
  301.5 76.1 all-gather.15
  460.5 114.6 reduce-scatter.15
  578.1 141.3 reduce-scatter.9
  726.1 151.2 reduce-scatter.7
  880.4 182.8 reduce-scatter.11
  1066.1 184.5 reduce-scatter.13
where the time goes:
time: 1270 us; the launch traced here: 1260 us
  waiting for transfers between devices  892 us (70%)
  blocking collectives  141 us (11%)
  local copies, waits for them, and re-layouts  122 us (10%)
  matrix products  72.3 us (6%)
  between operations  15.3 us (1%)
    reduce_scatter x1, waiting for transfers between devices, local(): lax.psum_scatter(proj_grad, ('dp', 'ctx'), scatter_dimension=0, tiled=True)  187 us
    reduce_scatter x1, waiting for transfers between devices, local(): lax.psum_scatter(fc_grad, ('dp', 'ctx'), scatter_dimension=0, tiled=True)  186 us
    reduce_scatter x1, waiting for transfers between devices, local(): lax.psum_scatter(qkv_grad, ('dp', 'ctx'), scatter_dimension=0, tiled=True)  158 us
    unnamed x11, waiting for transfers between devices  113 us
    unnamed x2, blocking collectives  84.3 us
    all_gather x1, waiting for transfers between devices, local(): lax.all_gather(shards[8], ('dp', 'ctx'), axis=0, tiled=True)  76.8 us
    all_gather x1, waiting for transfers between devices, local(): lax.all_gather(shards[10], ('dp', 'ctx'), axis=0, tiled=True)  74.2 us
    unnamed x125, local copies, waits for them, and re-layouts  63.8 us
  transfers between devices with their start and end apart: 10, of which 10 were waited for; matrix products, arithmetic and copies ran while one was open for 9% of the time, Pallas kernels for 0%

commit v1 on v0

v1 whole, which is shorter than its diff:
```python
import functools
import math

import jax
import jax.numpy as jnp
from jax import lax
from jax.experimental import pallas as pl
from jax.experimental.pallas import tpu as pltpu
from jax.sharding import PartitionSpec as P

HEADS = 16
EPSILON = 1e-05
QB = 256
F32, BF16 = jnp.float32, jnp.bfloat16
NT = (((1,), (1,)), ((), ()))
TN = (((0,), (0,)), ((), ()))


def attend_kernel(r, kc, a_ref, b_ref, idq_ref, idk_ref, o_ref, t_ref, acc, tot):
    part = lax.rem(lax.axis_index("ctx"), r) if r > 1 else 0
    length = b_ref.shape[0]

    def per_queries(lb, _):
        qs = pl.ds(pl.multiple_of(lb * QB, QB), QB)
        a = a_ref[qs, :] * 0.125
        idq = idq_ref[qs, :]
        acc[...] = jnp.zeros_like(acc)
        tot[...] = jnp.zeros_like(tot)

        def per_keys(kb, _):
            ks = pl.ds(pl.multiple_of(kb * kc, kc), kc)
            b = b_ref[ks, :]
            s = lax.dot_general(a, b, NT, preferred_element_type=F32)
            w = jnp.where(idk_ref[:, ks] <= idq, jnp.exp(s), 0.0)
            t = w[:, :128]
            for i in range(1, kc // 128):
                t = t + w[:, i * 128 : (i + 1) * 128]
            tot[...] += t
            acc[...] += jnp.dot(w.astype(BF16), b, preferred_element_type=F32)
            return 0

        reach = (lb * r + part + 2) * QB
        lax.fori_loop(0, jnp.minimum((reach + kc - 1) // kc, length // kc), per_keys, 0)
        t = jnp.sum(tot[...], axis=-1, keepdims=True)
        t_ref[qs, :] = t
        o_ref[qs, :] = acc[...] / t
        return 0

    lax.fori_loop(0, a_ref.shape[0] // QB, per_queries, 0)


def attend(r, a, b, idq, idk):
    rows = a.shape[0]
    return pl.pallas_call(
        functools.partial(attend_kernel, r, min(1024, b.shape[0])),
        out_shape=(jax.ShapeDtypeStruct((rows, 128), F32), jax.ShapeDtypeStruct((rows, 1), F32)),
        scratch_shapes=[pltpu.VMEM((QB, 128), F32), pltpu.VMEM((QB, 128), F32)],
        compiler_params=pltpu.CompilerParams(vmem_limit_bytes=48 << 20),
        name="attend",
    )(a, b, idq, idk)


def attend_back_kernel(r, kc, a_ref, b_ref, do_ref, ratio_ref, idq_ref, idk_ref, dq_ref, dkv_ref, acc):
    part = lax.rem(lax.axis_index("ctx"), r) if r > 1 else 0
    length = b_ref.shape[0]
    dkv_ref[...] = jnp.zeros_like(dkv_ref)

    def per_queries(lb, _):
        qs = pl.ds(pl.multiple_of(lb * QB, QB), QB)
        a = a_ref[qs, :]
        scaled = a * 0.125
        do = do_ref[qs, :]
        ado = jnp.concatenate([a, do], axis=0)
        idq = idq_ref[:, qs]
        ratio = ratio_ref[:, qs]
        acc[...] = jnp.zeros_like(acc)

        def per_keys(kb, _):
            ks = pl.ds(pl.multiple_of(kb * kc, kc), kc)
            b = b_ref[ks, :]
            s = lax.dot_general(b, scaled, NT, preferred_element_type=F32)
            w = jnp.where(idk_ref[ks, :] <= idq, jnp.exp(s), 0.0)
            p = lax.dot_general(b, do, NT, preferred_element_type=F32)
            g = (w * (p - ratio)).astype(BF16)
            gw = jnp.concatenate([g, w.astype(BF16)], axis=1)
            dkv_ref[ks, :] += jnp.dot(gw, ado, preferred_element_type=F32)
            acc[...] += lax.dot_general(g, b, TN, preferred_element_type=F32)
            return 0

        reach = (lb * r + part + 2) * QB
        lax.fori_loop(0, jnp.minimum((reach + kc - 1) // kc, length // kc), per_keys, 0)
        dq_ref[qs, :] = acc[...]
        return 0

    lax.fori_loop(0, a_ref.shape[0] // QB, per_queries, 0)


def attend_back(r, a, b, do, ratio, idq, idk):
    rows, length = a.shape[0], b.shape[0]
    return pl.pallas_call(
        functools.partial(attend_back_kernel, r, min(1024, length)),
        out_shape=(jax.ShapeDtypeStruct((rows, 128), F32), jax.ShapeDtypeStruct((length, 128), F32)),
        scratch_shapes=[pltpu.VMEM((QB, 128), F32)],
        compiler_params=pltpu.CompilerParams(vmem_limit_bytes=48 << 20),
        name="attend_back",
    )(a, b, do, ratio, idq, idk)


def normalize(rows):
    centred = rows - jnp.mean(rows, axis=-1, keepdims=True)
    rstd = lax.rsqrt(jnp.mean(centred * centred, axis=-1, keepdims=True) + EPSILON)
    return centred * rstd, rstd


def normalize_back(grad, normed, rstd):
    return rstd * (
        grad
        - jnp.mean(grad, axis=-1, keepdims=True)
        - normed * jnp.mean(grad * normed, axis=-1, keepdims=True)
    )


def gelu_both(u):
    c = math.sqrt(2.0 / math.pi)
    t = jnp.tanh(c * (u + 0.044715 * (u * u * u)))
    half = 0.5 * (1.0 + t)
    return u * half, half + 0.5 * u * (1.0 - t * t) * (c * (1.0 + 3.0 * 0.044715 * (u * u)))


def gather_ctx(v):
    return lax.all_gather(v, "ctx", axis=0, tiled=True)


def scatter_ctx(v):
    return lax.psum_scatter(v, "ctx", scatter_dimension=0, tiled=True).astype(F32)


def exchange_ctx(v):
    return lax.all_to_all(v, "ctx", 0, 0, tiled=True)


def dot(x, y, dims=(((1,), (0,)), ((), ()))):
    return lax.dot_general(x, y, dims, preferred_element_type=F32)


def local(n_dp, n, inputs, cotangent, block_ids, ln1_gain, ln1_bias, w_qkv, b_qkv, w_out, b_out, ln2_gain, ln2_bias, w_fc, b_fc, w_proj, b_proj):
    tokens, width = inputs.shape[1:]
    length = n * tokens
    rows = w_qkv.shape[0]
    units = w_proj.shape[0]
    r = n // HEADS
    hd = width // HEADS
    me = lax.axis_index("ctx")
    head, part = me // r, me % r

    small = jnp.concatenate([ln1_gain, ln1_bias, b_qkv, b_out, ln2_gain, ln2_bias, b_fc, b_proj])
    small = lax.all_gather(small, ("dp", "ctx"), axis=0).astype(F32)
    cuts, at = [], 0
    for v in (ln1_gain, ln1_bias, b_qkv, b_out, ln2_gain, ln2_bias, b_fc, b_proj):
        cuts.append(small[:, at : at + v.shape[0]])
        at += v.shape[0]
    g1, c1, bqv, bo, g2, c2, bf, bp = cuts
    g1, c1, bqv, bo, g2, c2, bp = (v.reshape(1, -1) for v in (g1, c1, bqv, bo, g2, c2, bp))
    bf = lax.dynamic_index_in_dim(bf.reshape(n_dp, n, units), me, 1, keepdims=False).reshape(1, -1)
    bqv = lax.dynamic_index_in_dim(bqv.reshape(2, HEADS, hd), head, 1, keepdims=False)
    zeros = jnp.zeros((hd,), F32)
    bias = jnp.concatenate([bqv[0], zeros, zeros, bqv[1]])[None]

    def spread(w):
        got = exchange_ctx(jnp.transpose(w, (1, 0, 2)))
        return lax.all_gather(got, "dp", axis=0, tiled=True).reshape(width, -1)

    wq = w_qkv.reshape(rows, 3, HEADS, 1, hd)
    wq = jnp.stack([wq[:, 0], jnp.zeros_like(wq[:, 0]), wq[:, 1], wq[:, 2]], axis=3)
    wq = jnp.broadcast_to(wq.reshape(rows, HEADS, 1, 4 * hd), (rows, HEADS, r, 4 * hd))
    wq = spread(wq.reshape(rows, n, 4 * hd))
    wf = spread(jnp.transpose(w_fc.reshape(rows, n_dp, n, units), (0, 2, 1, 3)).reshape(rows, n, n_dp * units))
    wp = lax.all_gather(w_proj, "dp", axis=0, tiled=True)
    wo = lax.all_gather(w_out, ("dp", "ctx"), axis=0, tiled=True)

    x_all = gather_ctx(inputs[0]).astype(F32)
    marks = gather_ctx(block_ids[0])
    normed, _ = normalize(x_all)
    first_low = (normed * g1 + c1).astype(BF16)
    qkv = (dot(first_low, wq) + bias).astype(BF16)
    a_all, b_all = qkv[:, : 2 * hd], qkv[:, 2 * hd :]

    def own_queries(v):
        if r == 1:
            return v
        split = v.reshape((length // QB // r, r, QB) + v.shape[1:])
        return lax.dynamic_index_in_dim(split, part, 1, keepdims=False).reshape((length // r,) + v.shape[1:])

    def all_queries(v):
        if r == 1:
            return v
        split = v.reshape((length // QB // r, 1, QB) + v.shape[1:])
        keep = (jnp.arange(r) == part).reshape((1, r, 1) + (1,) * (v.ndim - 1))
        return jnp.where(keep, split, 0).reshape((length,) + v.shape[1:])

    a, marks_q = own_queries(a_all), own_queries(marks)
    o, totals = attend(r, a, b_all, marks_q[:, None], marks[None])
    attended = o[:, hd:]
    low = all_queries(attended.astype(BF16))
    low = exchange_ctx(low.reshape(n, tokens, hd))
    low = low.reshape(HEADS, r, tokens, hd).sum(axis=1) if r > 1 else low
    attended_low = jnp.transpose(low, (1, 0, 2)).reshape(tokens, width)

    x = inputs[0].astype(F32)
    middle = x + dot(attended_low, wo) + bo
    n2, rstd2 = normalize(middle)
    second_low = gather_ctx((n2 * g2 + c2).astype(BF16))
    hidden = dot(second_low, wf) + bf
    active, slope = gelu_both(hidden)
    active_low = active.astype(BF16)
    output = middle + scatter_ctx(dot(active_low, wp).astype(BF16)) + bp

    dy_all = gather_ctx(cotangent[0])
    dy = cotangent[0].astype(F32)
    hidden_grad = slope * dot(dy_all, wp, NT)
    hidden_low = hidden_grad.astype(BF16)
    wp_grad = dot(active_low, dy_all, TN)
    wf_grad = dot(second_low, hidden_low, TN)
    bf_grad = jnp.sum(hidden_low.astype(F32), axis=0)
    second_grad = scatter_ctx(dot(hidden_low, wf, NT).astype(BF16))

    middle_grad = dy + normalize_back(second_grad * g2, n2, rstd2)
    branch_low = middle_grad.astype(BF16)
    wo_grad = dot(attended_low, branch_low, TN)
    attended_grad = dot(branch_low, wo, NT)
    sent = jnp.transpose(attended_grad.astype(BF16).reshape(tokens, HEADS, 1, hd), (1, 2, 0, 3))
    sent = jnp.broadcast_to(sent, (HEADS, r, tokens, hd)).reshape(n, tokens, hd)
    grad = own_queries(exchange_ctx(sent).reshape(length, hd)).astype(F32)
    ratio = jnp.sum(grad * attended, axis=-1, keepdims=True) / totals
    do = jnp.concatenate([jnp.zeros_like(grad), grad / totals], axis=1).astype(BF16)
    dq, dkv = attend_back(r, a, b_all, do, ratio.reshape(1, -1), marks_q[None], marks[:, None])
    dq = all_queries(dq[:, :hd]) * 0.125
    if r > 1:
        groups = [[h * r + i for i in range(r)] for h in range(HEADS)]
        dq, dkv = lax.psum((dq, dkv), "ctx", axis_index_groups=groups)
    mixed = jnp.concatenate([dq, jnp.zeros_like(dq), dkv[:, :hd] * 0.125, dkv[:, hd:]], axis=1).astype(BF16)
    if r > 1:
        mixed = jnp.where(part == 0, mixed, jnp.zeros_like(mixed))
    first_grad = scatter_ctx(dot(mixed, wq, NT).astype(BF16))
    wq_grad = dot(first_low, mixed, TN)
    mixed_sum = jnp.sum(mixed.astype(F32), axis=0)

    n1, rstd1 = normalize(x)
    input_grad = middle_grad + normalize_back(first_grad * g1, n1, rstd1)

    def collect(g):
        got = lax.psum_scatter(g.astype(BF16), "dp", scatter_dimension=0, tiled=True)
        return exchange_ctx(got.reshape(n, rows, -1)).astype(F32)

    wq_own = collect(wq_grad).reshape(HEADS, r, rows, 4, hd).sum(axis=1)
    wq_own = jnp.stack([wq_own[:, :, 0], wq_own[:, :, 2], wq_own[:, :, 3]], axis=1)
    wq_own = jnp.transpose(wq_own, (2, 1, 0, 3)).reshape(rows, 3 * width)
    wf_own = jnp.transpose(collect(wf_grad).reshape(n, rows, n_dp, units), (1, 2, 0, 3)).reshape(rows, -1)
    wp_own = lax.psum_scatter(wp_grad, "dp", scatter_dimension=0, tiled=True)
    wo_own = lax.psum_scatter(wo_grad.astype(BF16), ("dp", "ctx"), scatter_dimension=0, tiled=True).astype(F32)

    column = lambda v: jnp.sum(v, axis=0)
    hot = (jnp.arange(n) == me).astype(F32)[:, None]
    bqv_grad = jnp.stack([mixed_sum[:hd], mixed_sum[3 * hd :]])
    hot_head = (jnp.arange(HEADS) == head).astype(F32)[None, :, None]
    pieces = [
        column(first_grad * n1),
        column(first_grad),
        (hot_head * bqv_grad[:, None]).reshape(-1),
        column(branch_low.astype(F32)),
        column(second_grad * n2),
        column(second_grad),
        (hot[None] * bf_grad.reshape(n_dp, 1, units)).reshape(-1),
        column(dy),
    ]
    pieces = [v.reshape(n_dp * n, -1) for v in pieces]
    mine = lax.psum_scatter(jnp.concatenate(pieces, axis=1), ("dp", "ctx"), scatter_dimension=0, tiled=True)[0]
    outs, at = [], 0
    for v in pieces:
        outs.append(mine[at : at + v.shape[1]])
        at += v.shape[1]
    g1g, c1g, bqvg, bog, g2g, c2g, bfg, bpg = outs
    return (
        output.astype(BF16)[None], input_grad.astype(BF16)[None], g1g, c1g, wq_own, bqvg, wo_own, bog, g2g, c2g, wf_own, bfg, wp_own, bpg,
    )


def solution(mesh):
    both = ("dp", "ctx")
    act, vec, mat = P("dp", "ctx", None), P(both), P(both, None)
    return jax.shard_map(
        functools.partial(local, mesh.shape["dp"], mesh.shape["ctx"]),
        mesh=mesh,
        in_specs=(act, act, P("dp", "ctx"), vec, vec, mat, vec, mat, vec, vec, vec, mat, vec, mat, vec),
        out_specs=(act, act, vec, vec, mat, vec, mat, vec, vec, vec, mat, vec, mat, vec),
        check_vma=False,
    )
```

time: 1270 us -> 717 us (0.56)
  waiting for transfers between devices: 892 us -> 424 us
  local copies, waits for them, and re-layouts: 122 us -> 32.5 us
  matrix products: 72.3 us -> 42.2 us
  starting transfers between devices: 0.65 us -> 28 us
  Pallas kernels: 0 us -> 19.7 us
  other arithmetic: 8.62 us -> 21.5 us
    reduce_scatter x4 -> x7, waiting for transfers between devices: 589 us -> 324 us  [the longest x3 211 us: scatter_ctx(): lax.psum_scatter(v, 'ctx', scatter_dimension=0, tiled=True).astype(F32)]
    all_gather x5 -> x4, waiting for transfers between devices: 191 us -> 74.4 us  [the longest x3 64.3 us: gather_ctx(): return lax.all_gather(v, 'ctx', axis=0, tiled=True)]
    unnamed x11, waiting for transfers between devices: 113 us -> 2.03 us
    unnamed x125 -> x55, local copies, waits for them, and re-layouts: 63.8 us -> 9.97 us
    unnamed x2 -> x1, blocking collectives: 84.3 us -> 40.1 us
    all_gather x2 -> x5, blocking collectives: 56.5 us -> 93.1 us  [the longest x1 43.4 us: local(): small = lax.all_gather(small, ('dp', 'ctx'), axis=0).astype(F32)]
    dot_general x19 -> x12, matrix products: 72.3 us -> 42.2 us  [dot(): return lax.dot_general(x, y, dims, preferred_element_type=F32)]
    all_to_all x0 -> x6, starting transfers between devices: none -> 27.3 us  [exchange_ctx(): return lax.all_to_all(v, 'ctx', 0, 0, tiled=True)]
  transfers between devices with their start and end apart: 10 -> 17, of which waited for: 10 -> 12; matrix products, arithmetic and copies ran while one was open for 9% -> 10% of each run, Pallas kernels for 0% -> 3%
where the time goes in v1:
time: 717 us; the launch traced here: 716 us
  waiting for transfers between devices  424 us (59%)
  blocking collectives  133 us (19%)
  matrix products  42.2 us (6%)
  local copies, waits for them, and re-layouts  32.5 us (5%)
  starting transfers between devices  28 us (4%)
  other arithmetic  21.5 us (3%)
  Pallas kernels  19.7 us (3%)
  between operations  14.5 us (2%)
    reduce_scatter x3, waiting for transfers between devices, scatter_ctx(): lax.psum_scatter(v, 'ctx', scatter_dimension=0, tiled=True).astype(F32)  211 us
    reduce_scatter x1, waiting for transfers between devices, local(): lax.psum_scatter(wo_grad.astype(BF16), ('dp', 'ctx'), scatter_dimension=0...  112 us
    all_gather x3, waiting for transfers between devices, gather_ctx(): return lax.all_gather(v, 'ctx', axis=0, tiled=True)  64.3 us
    all_gather x1, blocking collectives, local(): small = lax.all_gather(small, ('dp', 'ctx'), axis=0).astype(F32)  43.4 us
    dot_general x12, matrix products, dot(): return lax.dot_general(x, y, dims, preferred_element_type=F32)  42.2 us
    unnamed x1, blocking collectives  40.1 us
    all_to_all x6, starting transfers between devices, exchange_ctx(): return lax.all_to_all(v, 'ctx', 0, 0, tiled=True)  27.3 us
    all_to_all x6, waiting for transfers between devices, exchange_ctx(): return lax.all_to_all(v, 'ctx', 0, 0, tiled=True)  24 us
  transfers between devices with their start and end apart: 17, of which 12 were waited for; matrix products, arithmetic and copies ran while one was open for 10% of the time, Pallas kernels for 3%

profile of v1, /device:TPU:0, one launch (start us, length us, event | category | flops | bytes accessed | tf_op | source)
XLA Modules:
  0.0 715.9 jit_solution(1536553210366420653)
XLA Ops:
  8.7 1.2 reshape.202
  11.8 7.4 %all-to-all-start = ((bf16[16,32,256]{2,1,0:T(8,128)(2,1)}), bf16[16,32,256]{2,1,0:T(8,128)(2,1)S(1)}, u32[]{:S(2)}, u32[]{:S(2)}) async-start(bf16[16,32,256]{2,1,0:T(8,128)(2,1)} %copy.95), calls=%async_computation | async-start | bytes 524288 | tf_op jit(solution)/shard_map/all_to_all | solution.py:139
  19.4 43.4 %all-gather.4 = bf16[32,1,384]{2,1,0:T(2,128)(2,1)S(1)} all-gather(bf16[1,1,384]{2,1,0:T(2,128)(2,1)S(1)} %reshape.242), channel_id=3, replica_groups=mesh['dp'=2,'ctx'=16] {'dp','ctx'}, dimensions={0}, use_global_device_ids=true | all-gather | bytes 25344 | tf_op jit(solution)/shard_map/all_gather | solution.py:157
  63.1 18.6 %all-gather.2.idk_ref.idq_ref = s32[1,2048]{1,0:T(1,128)S(1)} all-gather(s32[1,128]{1,0:T(1,128)S(1)} %copy-done.23), channel_id=4, replica_groups=mesh['dp'=2,'ctx'=16] {'ctx'}, dimensions={1}, use_global_device_ids=true | all-gather | bytes 8704 | tf_op jit(solution)/shard_map/all_gather | solution.py:131
  82.1 9.2 %all_gather.33 = bf16[32,32,256]{2,1,0:T(8,128)(2,1)S(1)} all-gather(bf16[16,32,256]{2,1,0:T(8,128)(2,1)S(1)} %all-to-all-done), channel_id=1, replica_groups=mesh['dp'=2,'ctx'=16] {'dp'}, dimensions={0}, use_global_device_ids=true | all-gather | bytes 786432 | tf_op jit(solution)/shard_map/all_gather | solution.py:171
  91.3 3.0 convert_reduce_fusion
  95.0 1.4 fusion.3
  96.4 1.7 fusion.6
  98.1 1.3 fusion.14
  100.2 7.7 %attend.1 = (f32[2048,128]{1,0:T(8,128)S(1)}, f32[2048,1]{1,0:T(8,128)S(1)}) custom-call(bf16[2048,128]{1,0:T(8,128)(2,1)S(1)} %get-tuple-element.38.a_ref, bf16[2048,128]{1,0:T(8,128)(2,1)S(1)} %get-tuple-element.37.b_ref, s32[2048,1]{1,0:T(8,128)S(1)} %copy.96.idq_ref.idk_ref, s32[1,2048]{1,0:T(1,128)S(1)} %all-gather.2.idk_ref.idq_ref), custom_call_target="tpu_custom_call" | custom-call | tf_op jit(solution)/shard_map/attend/pallas_call | solution.py:54
  107.9 1.1 copy-done
  109.0 1.0 slice.191
  110.0 2.0 copy.97
  111.9 4.2 all-to-all-start.1
  116.4 10.1 %all-gather.10.cloned.1.call-done = bf16[1024,1024]{1,0:T(8,128)(2,1)} async-done(((bf16[32,1024]{1,0:T(8,128)(2,1)}), bf16[1024,1024]{1,0:T(8,128)(2,1)}) %all-gather.10.cloned.1.call-update) | async-done | bytes 2097168 | tf_op jit(solution)/shard_map/all_gather | solution.py:179
  126.5 1.6 all-to-all-done.1
  128.1 2.2 fusion.61
  131.1 0.9 add_convert_fusion.1
  132.6 1.0 copy.112
  133.6 0.9 copy.124
  134.5 1.8 reshape.207
  136.3 1.7 copy.99
  138.1 4.2 all-to-all-start.2
  142.4 10.6 %all_gather.38 = bf16[256,1024]{1,0:T(8,128)(2,1)} all-gather(bf16[128,1024]{1,0:T(8,128)(2,1)} %param.28), channel_id=1, replica_groups=mesh['dp'=2,'ctx'=16] {'dp'}, dimensions={0}, use_global_device_ids=true | all-gather | bytes 786432 | tf_op jit(solution)/shard_map/all_gather | solution.py:178
  153.0 3.3 all-to-all-done.2
  156.3 11.4 %all_gather.37 = bf16[32,32,256]{2,1,0:T(8,128)(2,1)} all-gather(bf16[16,32,256]{2,1,0:T(8,128)(2,1)} %all-to-all-done.2), channel_id=1, replica_groups=mesh['dp'=2,'ctx'=16] {'dp'}, dimensions={0}, use_global_device_ids=true | all-gather | bytes 786432 | tf_op jit(solution)/shard_map/all_gather | solution.py:171
  167.6 18.1 %all-gather.12.cloned.1.call-done = bf16[2048,1024]{1,0:T(8,128)(2,1)} async-done(((bf16[128,1024]{1,0:T(8,128)(2,1)}), bf16[2048,1024]{1,0:T(8,128)(2,1)}) %all-gather.12.cloned.1.call-update) | async-done | bytes 4194320 | tf_op jit(solution)/shard_map/all_gather | solution.py:131
  185.7 4.9 convolution_add_fusion
  190.6 46.2 %all-gather.16.cloned.1.call-done = bf16[1,2048,1024]{2,1,0:T(8,128)(2,1)} async-done(((bf16[1,128,1024]{2,1,0:T(8,128)(2,1)}), bf16[1,2048,1024]{2,1,0:T(8,128)(2,1)}) %all-gather.16.cloned.1.call-update) | async-done | bytes 4194320 | tf_op jit(solution)/shard_map/all_gather | solution.py:131
  236.8 5.3 convert_reduce_fusion.1
  242.1 1.0 copy-done.10
  243.1 3.2 convolution_convert_fusion.1
  246.4 5.1 convolution_convert_fusion.2
  251.6 66.0 %reduce-scatter.10.cloned.1.call-done = bf16[128,1024]{1,0:T(8,128)(2,1)} async-done(((bf16[2048,1024]{1,0:T(8,128)(2,1)}), bf16[128,1024]{1,0:T(8,128)(2,1)}) %reduce-scatter.10.cloned.1.call-update) | async-done | bytes 262160 | tf_op jit(solution)/shard_map/reduce_scatter | solution.py:135
  317.6 1.4 fusion.49
  319.0 74.3 %reduce-scatter.8.cloned.1.call-done = bf16[128,1024]{1,0:T(8,128)(2,1)} async-done(((bf16[2048,1024]{1,0:T(8,128)(2,1)}), bf16[128,1024]{1,0:T(8,128)(2,1)}) %reduce-scatter.8.cloned.1.call-update) | async-done | bytes 262160 | tf_op jit(solution)/shard_map/reduce_scatter | solution.py:135
  393.3 2.4 convert_reduce_fusion.7
  396.5 1.5 convolution_convert_fusion.6
  398.0 1.8 copy.100
  399.8 4.2 all-to-all-start.3
  404.1 4.6 convolution_convert_fusion.4
  409.0 5.0 all-to-all-done.3
  414.0 2.2 copy.101
  416.2 1.9 fusion.28
  418.1 1.4 copy.102
  419.4 2.2 divide_reduce_fusion
  422.2 12.0 %attend_back.1 = (f32[2048,128]{1,0:T(8,128)S(1)}, f32[2048,128]{1,0:T(8,128)S(1)}) custom-call(bf16[2048,128]{1,0:T(8,128)(2,1)S(1)} %get-tuple-element.38.a_ref, bf16[2048,128]{1,0:T(8,128)(2,1)S(1)} %get-tuple-element.37.b_ref, bf16[2048,128]{1,0:T(8,128)(2,1)S(1)} %concatenate.22.do_ref, f32[1,2048]{1,0:T(1,128)S(1)} %bitcast.179, ...), custom_call_target="tpu_custom_call" | custom-call | tf_op jit(solution)/shard_map/attend_back/pallas_call | solution.py:100
  434.5 1.8 copy-done.9
  436.3 2.4 convolution_convert_fusion.5
  438.8 3.1 convolution_convert_fusion.3
  442.0 3.3 convolution_convert_fusion
  446.8 3.5 all-to-all-start.5
  450.4 5.2 fusion.7
  455.7 4.6 all-to-all-done.5
  460.9 1.1 copy.120
  462.2 3.8 all-to-all-start.4
  466.7 9.5 %all-to-all-done.4 = bf16[16,32,256]{2,1,0:T(8,128)(2,1)S(1)} async-done(((bf16[16,32,256]{2,1,0:T(8,128)(2,1)}), bf16[16,32,256]{2,1,0:T(8,128)(2,1)S(1)}, u32[]{:S(2)}, u32[]{:S(2)}) %all-to-all-start.4) | async-done | bytes 262176 | tf_op jit(solution)/shard_map/all_to_all | solution.py:139
  478.0 1.0 reshape.220
  479.0 112.5 %reduce-scatter.16.cloned.1.call-done = bf16[32,1024]{1,0:T(8,128)(2,1)} async-done(((bf16[1024,1024]{1,0:T(8,128)(2,1)}), bf16[32,1024]{1,0:T(8,128)(2,1)}) %reduce-scatter.16.cloned.1.call-update) | async-done | bytes 65552 | tf_op jit(solution)/shard_map/reduce_scatter | solution.py:260
  591.5 1.5 convert_element_type.131
  593.0 71.1 %reduce-scatter.12.cloned.1.call-done = bf16[128,1024]{1,0:T(8,128)(2,1)} async-done(((bf16[2048,1024]{1,0:T(8,128)(2,1)}), bf16[128,1024]{1,0:T(8,128)(2,1)}) %reduce-scatter.12.cloned.1.call-update) | async-done | bytes 262160 | tf_op jit(solution)/shard_map/reduce_scatter | solution.py:135
  664.1 1.3 fusion.50
  665.6 40.1 %all-reduce.1 = f32[32,384]{1,0:T(8,128)S(1)} all-reduce(f32[32,384]{1,0:T(8,128)S(1)} %concatenate.24), channel_id=9, replica_groups=mesh['dp'=2,'ctx'=16] {'dp','ctx'}, use_global_device_ids=true, to_apply=%region_22.23.clone | all-reduce | flops 12288 | bytes 98304
  707.5 1.9 fusion.52
  (142 shorter events, 16.4 us)
Async XLA Ops:
  7.2 84.1 %all-gather.14.cloned.1.call-start = ((), (), s32[]{:S(2)}) async-start(), calls=%async_computation.22 | async-start | bytes 4456448 | tf_op jit(solution)/shard_map/all_gather | solution.py:131
  7.9 118.6 %all-gather.10.cloned.1.call-start = ((), (), s32[]{:S(2)}) async-start(), calls=%async_computation.13 | async-start | bytes 2162688 | tf_op jit(solution)/shard_map/all_gather | solution.py:179
  9.9 9.2 %copy-start.15 = (bf16[32]{0:T(256)(128)(2,1)S(1)}, bf16[32]{0:T(256)(128)(2,1)}, u32[]{:S(2)}) copy-start(bf16[32]{0:T(256)(128)(2,1)} %param.18) | copy-start | bytes 196
  9.9 9.2 %copy-start.16 = (bf16[32]{0:T(256)(128)(2,1)S(1)}, bf16[32]{0:T(256)(128)(2,1)}, u32[]{:S(2)}) copy-start(bf16[32]{0:T(256)(128)(2,1)} %param.19) | copy-start | bytes 196
  10.0 9.2 %copy-start.17 = (bf16[64]{0:T(256)(128)(2,1)S(1)}, bf16[64]{0:T(256)(128)(2,1)}, u32[]{:S(2)}) copy-start(bf16[64]{0:T(256)(128)(2,1)} %param.21) | copy-start | bytes 388
  10.0 9.2 %copy-start.18 = (bf16[32]{0:T(256)(128)(2,1)S(1)}, bf16[32]{0:T(256)(128)(2,1)}, u32[]{:S(2)}) copy-start(bf16[32]{0:T(256)(128)(2,1)} %param.23) | copy-start | bytes 196
  10.0 9.2 %copy-start.19 = (bf16[32]{0:T(256)(128)(2,1)S(1)}, bf16[32]{0:T(256)(128)(2,1)}, u32[]{:S(2)}) copy-start(bf16[32]{0:T(256)(128)(2,1)} %param.24) | copy-start | bytes 196
  10.0 9.2 %copy-start.20 = (bf16[32]{0:T(256)(128)(2,1)S(1)}, bf16[32]{0:T(256)(128)(2,1)}, u32[]{:S(2)}) copy-start(bf16[32]{0:T(256)(128)(2,1)} %param.25) | copy-start | bytes 196
  10.0 9.2 %copy-start.21 = (bf16[128]{0:T(256)(128)(2,1)S(1)}, bf16[128]{0:T(256)(128)(2,1)}, u32[]{:S(2)}) copy-start(bf16[128]{0:T(256)(128)(2,1)} %param.27) | copy-start | bytes 772
  10.0 9.2 %copy-start.22 = (bf16[32]{0:T(256)(128)(2,1)S(1)}, bf16[32]{0:T(256)(128)(2,1)}, u32[]{:S(2)}) copy-start(bf16[32]{0:T(256)(128)(2,1)} %param.29) | copy-start | bytes 196
  10.1 53.0 %copy-start.23 = (s32[1,128]{1,0:T(1,128)S(1)}, s32[1,128]{1,0:T(1,128)}, u32[]{:S(2)}) copy-start(s32[1,128]{1,0:T(1,128)} %param.17) | copy-start | bytes 1540
  11.8 70.4 %all-to-all-start = ((bf16[16,32,256]{2,1,0:T(8,128)(2,1)}), bf16[16,32,256]{2,1,0:T(8,128)(2,1)S(1)}, u32[]{:S(2)}, u32[]{:S(2)}) async-start(bf16[16,32,256]{2,1,0:T(8,128)(2,1)} %copy.95), calls=%async_computation | async-start | bytes 524288 | tf_op jit(solution)/shard_map/all_to_all | solution.py:139
  91.3 6.8 copy-start.13
  91.3 3.7 copy-start.1
  98.1 2.0 copy-start.8
  100.1 28.0 %copy-start.4 = (bf16[1,128,1024]{2,1,0:T(8,128)(2,1)S(1)}, bf16[1,128,1024]{2,1,0:T(8,128)(2,1)}, u32[]{:S(2)}) copy-start(bf16[1,128,1024]{2,1,0:T(8,128)(2,1)} %param.15) | copy-start | bytes 786436
  107.9 1.1 copy-start
  111.9 16.2 %all-to-all-start.1 = ((bf16[16,128,64]{1,2,0:T(8,128)(2,1)}), bf16[16,128,64]{1,2,0:T(8,128)(2,1)}, u32[]{:S(2)}, u32[]{:S(2)}) async-start(bf16[16,128,64]{1,2,0:T(8,128)(2,1)} %copy.97), calls=%async_computation.1 | async-start | bytes 524288 | tf_op jit(solution)/shard_map/all_to_all | solution.py:139
  116.1 69.6 %all-gather.12.cloned.1.call-start = ((), (), s32[]{:S(2)}) async-start(), calls=%async_computation.14 | async-start | bytes 4456448 | tf_op jit(solution)/shard_map/all_gather | solution.py:131
  130.3 0.8 copy-start.2
  132.0 104.8 %all-gather.16.cloned.1.call-start = ((), (), s32[]{:S(2)}) async-start(), calls=%async_computation.23 | async-start | bytes 4456448 | tf_op jit(solution)/shard_map/all_gather | solution.py:131
  138.1 18.2 %all-to-all-start.2 = ((bf16[16,32,256]{2,1,0:T(8,128)(2,1)}), bf16[16,32,256]{2,1,0:T(8,128)(2,1)}, u32[]{:S(2)}, u32[]{:S(2)}) async-start(bf16[16,32,256]{2,1,0:T(8,128)(2,1)} %copy.99), calls=%async_computation.2 | async-start | bytes 524288 | tf_op jit(solution)/shard_map/all_to_all | solution.py:139
  142.3 175.3 %reduce-scatter.10.cloned.1.call-start = ((), (), s32[]{:S(2)}) async-start(), calls=%async_computation.16 | async-start | bytes 4456448 | tf_op jit(solution)/shard_map/reduce_scatter | solution.py:135
  236.8 6.3 copy-start.12
  242.1 1.0 copy-start.10
  246.4 146.9 %reduce-scatter.8.cloned.1.call-start = ((), (), s32[]{:S(2)}) async-start(), calls=%async_computation.15 | async-start | bytes 4456448 | tf_op jit(solution)/shard_map/reduce_scatter | solution.py:135
  393.3 3.2 copy-start.5
  395.7 0.8 copy-start.6
  399.8 14.2 %all-to-all-start.3 = ((bf16[16,128,64]{1,2,0:T(8,128)(2,1)}), bf16[16,128,64]{1,2,0:T(8,128)(2,1)}, u32[]{:S(2)}, u32[]{:S(2)}) async-start(bf16[16,128,64]{1,2,0:T(8,128)(2,1)} %bitcast.185), calls=%async_computation.5 | async-start | bytes 524288 | tf_op jit(solution)/shard_map/all_to_all | solution.py:139
  404.0 42.8 %reduce-scatter.18.cloned.1.call-start = ((), (), s32[]{:S(2)}) async-start(), calls=%async_computation.20 | async-start | bytes 786432 | tf_op jit(solution)/shard_map/reduce_scatter | solution.py:252
  408.8 53.5 %reduce-scatter.14.cloned.1.call-start = ((), (), s32[]{:S(2)}) async-start(), calls=%async_computation.18 | async-start | bytes 786432 | tf_op jit(solution)/shard_map/reduce_scatter | solution.py:252
  418.1 3.5 copy-start.3
  434.1 2.2 copy-start.9
  436.3 2.5 copy-start.7
  438.8 3.2 copy-start.14
  438.8 152.7 %reduce-scatter.16.cloned.1.call-start = ((), (), s32[]{:S(2)}) async-start(), calls=%async_computation.19 | async-start | bytes 2162688 | tf_op jit(solution)/shard_map/reduce_scatter | solution.py:260
  441.9 222.1 %reduce-scatter.12.cloned.1.call-start = ((), (), s32[]{:S(2)}) async-start(), calls=%async_computation.17 | async-start | bytes 4456448 | tf_op jit(solution)/shard_map/reduce_scatter | solution.py:135
  445.3 0.9 copy-start.11
  446.8 13.6 %all-to-all-start.5 = ((bf16[16,32,256]{2,1,0:T(8,128)(2,1)}), bf16[16,32,256]{2,1,0:T(8,128)(2,1)S(1)}, u32[]{:S(2)}, u32[]{:S(2)}) async-start(bf16[16,32,256]{2,1,0:T(8,128)(2,1)} %bitcast.199), calls=%async_computation.11 | async-start | bytes 524288 | tf_op jit(solution)/shard_map/all_to_all | solution.py:139
  450.3 259.1 %reduce-scatter.20.cloned.1.call-start = ((), (), s32[]{:S(2)}) async-start(), calls=%async_computation.21 | async-start | bytes 1572864 | tf_op jit(solution)/shard_map/reduce_scatter | solution.py:259
  462.2 14.0 %all-to-all-start.4 = ((bf16[16,32,256]{2,1,0:T(8,128)(2,1)}), bf16[16,32,256]{2,1,0:T(8,128)(2,1)S(1)}, u32[]{:S(2)}, u32[]{:S(2)}) async-start(bf16[16,32,256]{2,1,0:T(8,128)(2,1)} %bitcast.200), calls=%async_computation.8 | async-start | bytes 524288 | tf_op jit(solution)/shard_map/all_to_all | solution.py:139
Sparse Core Ops, SparseCore 0:
  10.2 57.4 all-gather.13
  70.5 55.9 all-gather.9
  132.2 53.5 all-gather.11
  187.7 49.0 all-gather.15
  246.5 71.0 reduce-scatter.9
  321.8 71.4 reduce-scatter.7
  408.9 15.7 reduce-scatter.17
  438.9 12.8 reduce-scatter.13
  454.0 137.4 reduce-scatter.15
  595.7 68.3 reduce-scatter.11
  666.9 19.5 reduce-scatter.19

commit v2 on v1

--- a/solution.py
+++ b/solution.py
@@ -14,6 +14,266 @@
 F32, BF16 = jnp.float32, jnp.bfloat16
 NT = (((1,), (1,)), ((), ()))
 TN = (((0,), (0,)), ((), ()))
+MESH = pl.DeviceIdType.MESH
+DMA = pltpu.SemaphoreType.DMA
+
+
+class Line:
+    def __init__(self, n):
+        self.n, self.ys = n, n // 8
+        me = lax.axis_index("ctx")
+        self.z, self.y, self.c = me // (2 * self.ys), me // 2 % self.ys, me % 2
+        high = self.z // 2
+        self.slots = [3 - 3 * high, 2 - high, self.z + 1 - 2 * (self.z % 2), self.z]
+        self.inner = (self.z == 1) | (self.z == 2)
+        self.outer = (self.z == 0) | (self.z == 3)
+        self.side = (self.z + 1) // 2 % 2
+        self.near = self.at(self.slots[2], self.y, self.c)
+        self.far = self.at(self.z + 1 - 2 * high, self.y, self.c)
+        self.core = self.at(self.z, self.y, 1 - self.c)
+
+    def at(self, z, y, c):
+        return {"ctx": (z * self.ys + y) * 2 + c}
+
+    def others(self):
+        return [(self.y + d) % self.ys for d in range(1, self.ys)]
+
+    def greet(self):
+        peers = [self.core, self.near] + [self.at(self.z, y, self.c) for y in self.others()]
+        barrier = pltpu.get_barrier_semaphore()
+        for peer in peers:
+            pl.semaphore_signal(barrier, inc=1, device_id=peer, device_id_type=MESH)
+
+        @pl.when(self.inner)
+        def _():
+            pl.semaphore_signal(barrier, inc=1, device_id=self.far, device_id_type=MESH)
+
+        pl.semaphore_wait(barrier, len(peers) + self.side)
+
+
+def remote(src, dst, send, recv, peer):
+    return pltpu.make_async_remote_copy(src_ref=src, dst_ref=dst, send_sem=send, recv_sem=recv, device_id=peer, device_id_type=MESH)
+
+
+class LineGather:
+    def __init__(self, line, buf, sems):
+        self.l, self.buf = line, buf
+        self.zs, self.zr, self.ys, self.yr, self.ks, self.kr = sems
+
+    @staticmethod
+    def sems(n):
+        ys = n // 8
+        return [DMA((5,)), DMA((3,)), DMA((ys - 1, 4)), DMA((ys - 1, 4)), DMA((ys, 4)), DMA((ys, 4))]
+
+    def move(self, z, y, c, send, recv, peer):
+        ref = self.buf.at[z, y, c]
+        return remote(ref, ref, send, recv, peer)
+
+    def zcopy(self, i):
+        l = self.l
+        slot, peer, into = [(3, l.near, 0), (3, l.far, 1), (2, l.far, 2), (1, l.near, 1), (0, l.near, 2)][i]
+        return self.move(l.slots[slot], l.y, l.c, self.zs.at[i], self.zr.at[into], peer)
+
+    def ycopy(self, d, slot):
+        l = self.l
+        return self.move(l.slots[slot], l.y, l.c, self.ys.at[d, slot], self.yr.at[d, slot], l.at(l.z, l.others()[d], l.c))
+
+    def kcopy(self, d, slot):
+        l = self.l
+        y = l.y if d == 0 else (l.y + l.ys - d) % l.ys
+        return self.move(l.slots[slot], y, l.c, self.ks.at[d, slot], self.kr.at[d, slot], l.core)
+
+    def spread(self, slot):
+        for d in range(self.l.ys - 1):
+            self.ycopy(d, slot).start()
+        self.kcopy(0, slot).start()
+
+    def start(self):
+        self.zcopy(0).start()
+
+        @pl.when(self.l.inner)
+        def _():
+            self.zcopy(1).start()
+
+        self.spread(3)
+
+    def z_step(self, r):
+        self.zcopy((0, 3, 4)[r]).wait_recv()
+
+        @pl.when(self.l.inner)
+        def _():
+            self.zcopy(2 + r).start()
+
+        self.spread(2 - r)
+
+    def y_step(self, slot):
+        for d in range(self.l.ys - 1):
+            self.ycopy(d, slot).wait_recv()
+            self.kcopy(d + 1, slot).start()
+
+    def run(self):
+        self.start()
+        for r in range(3):
+            self.z_step(r)
+            self.y_step(3 - r)
+        self.y_step(0)
+
+    def core_wait(self, slot):
+        for d in range(self.l.ys):
+            self.kcopy(d, slot).wait_recv()
+
+    def finish(self):
+        self.zcopy(0).wait_send()
+
+        @pl.when(self.l.inner)
+        def _():
+            for i in range(1, 5):
+                self.zcopy(i).wait_send()
+
+        for slot in range(4):
+            for d in range(self.l.ys - 1):
+                self.ycopy(d, slot).wait_send()
+            for d in range(self.l.ys):
+                self.kcopy(d, slot).wait_send()
+
+
+class LineScatter:
+    def __init__(self, line, acc, kbuf, ybuf, zbuf, sems):
+        self.l, self.acc, self.kbuf, self.ybuf, self.zbuf = line, acc, kbuf, ybuf, zbuf
+        self.zs, self.zr, self.ys, self.yr, self.ks, self.kr = sems
+
+    @staticmethod
+    def sems(n):
+        ys = n // 8
+        return [DMA((3,)), DMA((2, 3)), DMA((ys - 1, 4)), DMA((ys - 1, 4)), DMA((ys, 4)), DMA((ys, 4))]
+
+    @staticmethod
+    def scratch(n, rows, cols):
+        ys = n // 8
+        return [pltpu.VMEM((4, ys, rows, cols), BF16), pltpu.VMEM((ys - 1, 4, rows, cols), BF16), pltpu.VMEM((2, 3, rows, cols), BF16)]
+
+    def y_of(self, d):
+        return self.l.y if d == 0 else self.l.others()[d - 1]
+
+    def kcopy(self, d, slot):
+        l = self.l
+        z, y = l.slots[slot], self.y_of(d)
+        return remote(self.acc.at[z, y, 1 - l.c], self.kbuf.at[z, y], self.ks.at[d, slot], self.kr.at[d, slot], l.core)
+
+    def ycopy(self, d, slot):
+        l = self.l
+        z, y = l.slots[slot], self.y_of(d + 1)
+        return remote(self.acc.at[z, y, l.c], self.ybuf.at[d, slot], self.ys.at[d, slot], self.yr.at[d, slot], l.at(l.z, y, l.c))
+
+    def zcopy(self, slot):
+        l = self.l
+        return remote(self.acc.at[l.slots[slot], l.y, l.c], self.zbuf.at[l.side, slot], self.zs.at[slot], self.zr.at[l.side, slot], l.far if slot < 2 else l.near)
+
+    def zwait(self, side, slot):
+        buf = self.zbuf.at[side, slot]
+        remote(buf, buf, self.zs.at[slot], self.zr.at[side, slot], self.l.near).wait_recv()
+        return self.zbuf[side, slot].astype(F32)
+
+    def own(self, slot):
+        return (self.l.slots[slot], self.l.y, self.l.c)
+
+    def core_start(self, slot):
+        for d in range(self.l.ys - 1, -1, -1):
+            self.kcopy(d, slot).start()
+
+    def core_step(self, slot):
+        l = self.l
+        for d in list(range(1, l.ys)) + [0]:
+            z, y = l.slots[slot], self.y_of(d)
+            self.kcopy(d, slot).wait_recv()
+            self.acc[z, y, l.c] = (self.acc[z, y, l.c].astype(F32) + self.kbuf[z, y].astype(F32)).astype(BF16)
+            if d > 0:
+                self.ycopy(d - 1, slot).start()
+
+    def y_sum(self, slot):
+        total = self.acc[self.own(slot)].astype(F32)
+        for d in range(self.l.ys - 1):
+            self.ycopy(d, slot).wait_recv()
+            total = total + self.ybuf[d, slot].astype(F32)
+        return total
+
+    def z_step(self, slot):
+        l, own = self.l, self.own(slot)
+        total = self.y_sum(slot)
+        self.acc[own] = total.astype(BF16)
+        @pl.when(l.inner)
+        def _():
+            self.acc[own] = (self.acc[own].astype(F32) + self.zwait(*((0, slot) if slot < 2 else (1, 0)))).astype(BF16)
+
+        self.zcopy(slot).start()
+
+    def last(self, out):
+        l = self.l
+        out[...] = self.y_sum(3)
+
+        @pl.when(l.inner)
+        def _():
+            out[...] += self.zwait(0, 2) + self.zwait(1, 1)
+
+        @pl.when(l.outer)
+        def _():
+            out[...] += self.zwait(1, 2)
+
+    def finish(self):
+        for slot in range(4):
+            for d in range(self.l.ys):
+                self.kcopy(d, slot).wait_send()
+            for d in range(self.l.ys - 1):
+                self.ycopy(d, slot).wait_send()
+        for slot in range(3):
+            self.zcopy(slot).wait_send()
+
+
+def line_gather_kernel(n, x_ref, o_ref, *sems):
+    line = Line(n)
+    g = LineGather(line, o_ref, sems)
+    line.greet()
+    o_ref[line.z, line.y, line.c] = x_ref[...]
+    g.run()
+    for slot in range(4):
+        g.core_wait(slot)
+    g.finish()
+
+
+def line_gather(cid, n, x):
+    out = pl.pallas_call(
+        functools.partial(line_gather_kernel, n),
+        out_shape=jax.ShapeDtypeStruct((4, n // 8, 2) + x.shape, x.dtype),
+        in_specs=[pl.BlockSpec(memory_space=pltpu.VMEM)], out_specs=pl.BlockSpec(memory_space=pltpu.VMEM),
+        scratch_shapes=LineGather.sems(n),
+        compiler_params=pltpu.CompilerParams(collective_id=cid, has_side_effects=True, vmem_limit_bytes=56 << 20), name=f"line_gather{cid}")(x)
+    return out.reshape((-1,) + x.shape[1:])
+
+
+def line_scatter_kernel(n, v_ref, o_ref, acc, kbuf, ybuf, zbuf, *sems):
+    line = Line(n)
+    s = LineScatter(line, acc, kbuf, ybuf, zbuf, sems)
+    acc[...] = v_ref[...]
+    line.greet()
+    for slot in range(4):
+        s.core_start(slot)
+    for slot in range(4):
+        s.core_step(slot)
+    for slot in range(3):
+        s.z_step(slot)
+    s.last(o_ref)
+    s.finish()
+
+
+def line_scatter(cid, n, v):
+    rows, cols = v.shape[0] // n, v.shape[1]
+    v = v.reshape((4, n // 8, 2, rows, cols))
+    return pl.pallas_call(
+        functools.partial(line_scatter_kernel, n),
+        out_shape=jax.ShapeDtypeStruct((rows, cols), F32),
+        in_specs=[pl.BlockSpec(memory_space=pltpu.VMEM)], out_specs=pl.BlockSpec(memory_space=pltpu.VMEM),
+        scratch_shapes=[pltpu.VMEM(v.shape, BF16)] + LineScatter.scratch(n, rows, cols) + LineScatter.sems(n),
+        compiler_params=pltpu.CompilerParams(collective_id=cid, has_side_effects=True, vmem_limit_bytes=56 << 20), name=f"line_scatter{cid}")(v)
 
 
 def attend_kernel(r, kc, a_ref, b_ref, idq_ref, idk_ref, o_ref, t_ref, acc, tot):
@@ -125,14 +385,6 @@
     t = jnp.tanh(c * (u + 0.044715 * (u * u * u)))
     half = 0.5 * (1.0 + t)
     return u * half, half + 0.5 * u * (1.0 - t * t) * (c * (1.0 + 3.0 * 0.044715 * (u * u)))
-
-
-def gather_ctx(v):
-    return lax.all_gather(v, "ctx", axis=0, tiled=True)
-
-
-def scatter_ctx(v):
-    return lax.psum_scatter(v, "ctx", scatter_dimension=0, tiled=True).astype(F32)
 
 
 def exchange_ctx(v):
@@ -178,8 +430,8 @@
     wp = lax.all_gather(w_proj, "dp", axis=0, tiled=True)
     wo = lax.all_gather(w_out, ("dp", "ctx"), axis=0, tiled=True)
 
-    x_all = gather_ctx(inputs[0]).astype(F32)
-    marks = gather_ctx(block_ids[0])
+    x_all = line_gather(1, n, inputs[0]).astype(F32)
+    marks = lax.all_gather(block_ids[0], "ctx", axis=0, tiled=True)
     normed, _ = normalize(x_all)
     first_low = (normed * g1 + c1).astype(BF16)
     qkv = (dot(first_low, wq) + bias).astype(BF16)
@@ -209,20 +461,20 @@
     x = inputs[0].astype(F32)
     middle = x + dot(attended_low, wo) + bo
     n2, rstd2 = normalize(middle)
-    second_low = gather_ctx((n2 * g2 + c2).astype(BF16))
+    second_low = line_gather(2, n, (n2 * g2 + c2).astype(BF16))
     hidden = dot(second_low, wf) + bf
     active, slope = gelu_both(hidden)
     active_low = active.astype(BF16)
-    output = middle + scatter_ctx(dot(active_low, wp).astype(BF16)) + bp
-
-    dy_all = gather_ctx(cotangent[0])
+    output = middle + line_scatter(3, n, dot(active_low, wp).astype(BF16)) + bp
+
+    dy_all = line_gather(4, n, cotangent[0])
     dy = cotangent[0].astype(F32)
     hidden_grad = slope * dot(dy_all, wp, NT)
     hidden_low = hidden_grad.astype(BF16)
     wp_grad = dot(active_low, dy_all, TN)
     wf_grad = dot(second_low, hidden_low, TN)
     bf_grad = jnp.sum(hidden_low.astype(F32), axis=0)
-    second_grad = scatter_ctx(dot(hidden_low, wf, NT).astype(BF16))
+    second_grad = line_scatter(5, n, dot(hidden_low, wf, NT).astype(BF16))
 
     middle_grad = dy + normalize_back(second_grad * g2, n2, rstd2)
     branch_low = middle_grad.astype(BF16)
@@ -241,7 +493,7 @@
     mixed = jnp.concatenate([dq, jnp.zeros_like(dq), dkv[:, :hd] * 0.125, dkv[:, hd:]], axis=1).astype(BF16)
     if r > 1:
         mixed = jnp.where(part == 0, mixed, jnp.zeros_like(mixed))
-    first_grad = scatter_ctx(dot(mixed, wq, NT).astype(BF16))
+    first_grad = line_scatter(6, n, dot(mixed, wq, NT).astype(BF16))
     wq_grad = dot(first_low, mixed, TN)
     mixed_sum = jnp.sum(mixed.astype(F32), axis=0)
 

time: 717 us -> 569 us (0.79); the launches traced: 716 us -> 560 us
  waiting for transfers between devices: 424 us -> 65.4 us
  Pallas kernels: 19.7 us -> 228 us
    reduce_scatter x3 -> x0, waiting for transfers between devices: 211 us -> none  [scatter_ctx(): lax.psum_scatter(v, 'ctx', scatter_dimension=0, tiled=True).astype(F32)]
    pallas_call x0 -> x6, Pallas kernels: none -> 209 us  [the longest x3 108 us: line_scatter(): pl.pallas_call(functools.partial(line_scatter_kernel, n), out_shape=jax.S...]
    reduce_scatter x1, waiting for transfers between devices: 112 us -> 35.5 us  [local(): lax.psum_scatter(wo_grad.astype(BF16), ('dp', 'ctx'), scatter_dimension=0...]
    all_gather x3 -> x0, waiting for transfers between devices: 64.3 us -> none  [gather_ctx(): return lax.all_gather(v, 'ctx', axis=0, tiled=True)]
    reduce_scatter x1, waiting for transfers between devices: 0.01 us -> 19.1 us  [local(): wp_own = lax.psum_scatter(wp_grad, 'dp', scatter_dimension=0, tiled=True)]
    all_to_all x6, waiting for transfers between devices: 24 us -> 10 us  [exchange_ctx(): return lax.all_to_all(v, 'ctx', 0, 0, tiled=True)]
    all_gather x1, waiting for transfers between devices: 10.1 us -> 0.01 us  [local(): wo = lax.all_gather(w_out, ('dp', 'ctx'), axis=0, tiled=True)]
  transfers between devices with their start and end apart: 17 -> 11, of which waited for: 12 -> 4; matrix products, arithmetic and copies ran while one was open for 10% -> 11% of each run, Pallas kernels for 3% -> 23%
where the time goes in v2:
time: 569 us; the launch traced here: 560 us
  Pallas kernels  228 us (40%)
  blocking collectives  130 us (23%)
  waiting for transfers between devices  65.4 us (11%)
  matrix products  37.5 us (7%)
  starting transfers between devices  30.8 us (5%)
  local copies, waits for them, and re-layouts  26.9 us (5%)
  other arithmetic  26.3 us (5%)
  between operations  15 us (3%)
    pallas_call x3, Pallas kernels, line_scatter(): pl.pallas_call(functools.partial(line_scatter_kernel, n), out_shape=jax.S...  108 us
    pallas_call x3, Pallas kernels, line_gather(): pl.pallas_call(functools.partial(line_gather_kernel, n), out_shape=jax.Sh...  101 us
    all_gather x1, blocking collectives, local(): small = lax.all_gather(small, ('dp', 'ctx'), axis=0).astype(F32)  42.2 us
    unnamed x1, blocking collectives  41.5 us
    dot_general x12, matrix products, dot(): return lax.dot_general(x, y, dims, preferred_element_type=F32)  37.5 us
    reduce_scatter x1, waiting for transfers between devices, local(): lax.psum_scatter(wo_grad.astype(BF16), ('dp', 'ctx'), scatter_dimension=0...  35.5 us
    all_to_all x6, starting transfers between devices, exchange_ctx(): return lax.all_to_all(v, 'ctx', 0, 0, tiled=True)  30.4 us
    all_gather x2, blocking collectives, spread(): return lax.all_gather(got, 'dp', axis=0, tiled=True).reshape(width, -1)  19.8 us
  transfers between devices with their start and end apart: 11, of which 4 were waited for; matrix products, arithmetic and copies ran while one was open for 11% of the time, Pallas kernels for 23%

profile of v2, /device:TPU:0, one launch (start us, length us, event | category | flops | bytes accessed | tf_op | source)
XLA Modules:
  0.0 560.4 jit_solution(1538204905629846704)
XLA Ops:
  7.2 0.7 all-gather.5.cloned.1.call-update
  7.9 1.2 reshape.261
  10.3 0.8 copy.95
  11.1 7.4 %all-to-all-start = ((bf16[16,32,256]{2,1,0:T(8,128)(2,1)}), bf16[16,32,256]{2,1,0:T(8,128)(2,1)S(1)}, u32[]{:S(2)}, u32[]{:S(2)}) async-start(bf16[16,32,256]{2,1,0:T(8,128)(2,1)} %copy.95), calls=%async_computation | async-start | bytes 524288 | tf_op jit(solution)/shard_map/all_to_all | solution.py:391
  18.6 42.2 %all-gather.2 = bf16[32,1,384]{2,1,0:T(2,128)(2,1)S(1)} all-gather(bf16[1,1,384]{2,1,0:T(2,128)(2,1)S(1)} %reshape.302), channel_id=2, replica_groups=mesh['dp'=2,'ctx'=16] {'dp','ctx'}, dimensions={0}, use_global_device_ids=true | all-gather | bytes 25344 | tf_op jit(solution)/shard_map/all_gather | solution.py:409
  61.6 0.8 copy.99
  62.4 17.3 %all-gather.1.idk_ref.idq_ref = s32[1,2048]{1,0:T(1,128)S(1)} all-gather(s32[1,128]{1,0:T(1,128)S(1)} %copy-done.30), channel_id=3, replica_groups=mesh['dp'=2,'ctx'=16] {'ctx'}, dimensions={1}, use_global_device_ids=true | all-gather | bytes 8704 | tf_op jit(solution)/shard_map/all_gather | solution.py:434
  80.0 32.5 %line_gather1.1 = bf16[4,2,2,128,1024]{4,3,2,1,0:T(8,128)(2,1)} custom-call(bf16[128,1024]{1,0:T(8,128)(2,1)} %bitcast.148), custom_call_target="tpu_custom_call" | custom-call | tf_op jit(solution)/shard_map/line_gather1/pallas_call | solution.py:244
  112.7 3.0 convert_reduce_fusion
  116.1 1.4 multiply_reduce_fusion
  117.5 3.0 add_convert_fusion
  120.5 4.2 all-to-all-start.2
  124.7 9.2 %all_gather.23 = bf16[32,32,256]{2,1,0:T(8,128)(2,1)S(1)} all-gather(bf16[16,32,256]{2,1,0:T(8,128)(2,1)S(1)} %all-to-all-done), channel_id=1, replica_groups=mesh['dp'=2,'ctx'=16] {'dp'}, dimensions={0}, use_global_device_ids=true | all-gather | bytes 786432 | tf_op jit(solution)/shard_map/all_gather | solution.py:423
  133.9 0.8 copy-done.17
  134.7 3.4 fusion.4
  138.2 7.7 %attend.1 = (f32[2048,128]{1,0:T(8,128)S(1)}, f32[2048,1]{1,0:T(8,128)S(1)}) custom-call(bf16[2048,128]{1,0:T(8,128)(2,1)S(1)} %get-tuple-element.38.a_ref, bf16[2048,128]{1,0:T(8,128)(2,1)S(1)} %get-tuple-element.37.b_ref, s32[2048,1]{1,0:T(8,128)S(1)} %copy.96.idq_ref.idk_ref, s32[1,2048]{1,0:T(1,128)S(1)} %all-gather.1.idk_ref.idq_ref), custom_call_target="tpu_custom_call" | custom-call | tf_op jit(solution)/shard_map/attend/pallas_call | solution.py:314
  145.9 1.0 copy-done
  146.9 1.0 slice.191
  147.9 1.9 copy.97
  149.8 5.8 %all-to-all-start.1 = ((bf16[16,128,64]{1,2,0:T(8,128)(2,1)}), bf16[16,128,64]{1,2,0:T(8,128)(2,1)}, u32[]{:S(2)}, u32[]{:S(2)}) async-start(bf16[16,128,64]{1,2,0:T(8,128)(2,1)} %copy.97), calls=%async_computation.1 | async-start | bytes 524288 | tf_op jit(solution)/shard_map/all_to_all | solution.py:391
  156.6 36.9 %line_gather4.1 = bf16[4,2,2,128,1024]{4,3,2,1,0:T(8,128)(2,1)} custom-call(bf16[128,1024]{1,0:T(8,128)(2,1)} %bitcast.160), custom_call_target="tpu_custom_call" | custom-call | tf_op jit(solution)/shard_map/line_gather4/pallas_call | solution.py:244
  193.5 0.7 constant_dynamic-slice_fusion.1
  194.3 9.4 %all_gather.27 = bf16[256,1024]{1,0:T(8,128)(2,1)} all-gather(bf16[128,1024]{1,0:T(8,128)(2,1)S(1)} %copy-done.20), channel_id=1, replica_groups=mesh['dp'=2,'ctx'=16] {'dp'}, dimensions={0}, use_global_device_ids=true | all-gather | bytes 786432 | tf_op jit(solution)/shard_map/all_gather | solution.py:430
  203.6 10.6 %all_gather.26 = bf16[32,32,256]{2,1,0:T(8,128)(2,1)} all-gather(bf16[16,32,256]{2,1,0:T(8,128)(2,1)} %all-to-all-done.2), channel_id=1, replica_groups=mesh['dp'=2,'ctx'=16] {'dp'}, dimensions={0}, use_global_device_ids=true | all-gather | bytes 786432 | tf_op jit(solution)/shard_map/all_gather | solution.py:423
  214.2 2.2 fusion.39
  216.7 0.9 add_convert_fusion.2.x_ref
  217.6 31.4 %line_gather2.1 = bf16[4,2,2,128,1024]{4,3,2,1,0:T(8,128)(2,1)} custom-call(bf16[128,1024]{1,0:T(8,128)(2,1)} %add_convert_fusion.2.x_ref), custom_call_target="tpu_custom_call" | custom-call | tf_op jit(solution)/shard_map/line_gather2/pallas_call | solution.py:244
  249.0 3.5 convolution_add_fusion
  252.5 3.4 convolution_convert_fusion.2
  255.9 33.6 %line_scatter3.1 = f32[128,1024]{1,0:T(8,128)} custom-call(bf16[4,2,2,128,1024]{4,3,2,1,0:T(8,128)(2,1)} %bitcast.151), custom_call_target="tpu_custom_call" | custom-call | tf_op jit(solution)/shard_map/line_scatter3/pallas_call | solution.py:271
  289.6 4.0 convert_reduce_fusion.1
  293.6 3.2 convolution_convert_fusion.1
  296.9 36.3 %line_scatter5.1 = f32[128,1024]{1,0:T(8,128)} custom-call(bf16[4,2,2,128,1024]{4,3,2,1,0:T(8,128)(2,1)} %bitcast.147), custom_call_target="tpu_custom_call" | custom-call | tf_op jit(solution)/shard_map/line_scatter5/pallas_call | solution.py:271
  333.2 1.5 multiply_reduce_fusion.1
  334.6 2.0 convert_reduce_fusion.5
  336.7 0.8 copy-done.5
  337.5 1.5 convolution_convert_fusion.6
  339.0 1.8 copy.100
  340.8 4.2 all-to-all-start.3
  345.3 4.7 fusion.3
  350.1 2.1 convolution_convert_fusion.4
  352.3 2.8 all-to-all-done.3
  355.0 2.1 copy.101
  357.2 1.9 fusion.16
  359.1 1.4 copy.102
  360.4 2.2 divide_reduce_fusion
  363.2 12.0 %attend_back.1 = (f32[2048,128]{1,0:T(8,128)S(1)}, f32[2048,128]{1,0:T(8,128)S(1)}) custom-call(bf16[2048,128]{1,0:T(8,128)(2,1)S(1)} %get-tuple-element.38.a_ref, bf16[2048,128]{1,0:T(8,128)(2,1)S(1)} %get-tuple-element.37.b_ref, bf16[2048,128]{1,0:T(8,128)(2,1)S(1)} %concatenate.22.do_ref, f32[1,2048]{1,0:T(1,128)S(1)} %bitcast.146, ...), custom_call_target="tpu_custom_call" | custom-call | tf_op jit(solution)/shard_map/attend_back/pallas_call | solution.py:360
  375.5 1.8 copy-done.8
  377.3 2.4 convolution_convert_fusion.5
  379.8 3.0 convolution_convert_fusion.3
  383.6 5.3 fusion.35
  389.0 3.3 convolution_convert_fusion
  392.3 38.0 %line_scatter6.1 = f32[128,1024]{1,0:T(8,128)} custom-call(bf16[4,2,2,128,1024]{4,3,2,1,0:T(8,128)(2,1)} %bitcast.150), custom_call_target="tpu_custom_call" | custom-call | tf_op jit(solution)/shard_map/line_scatter6/pallas_call | solution.py:271
  430.4 1.4 fusion.27
  432.4 3.5 all-to-all-start.5
  436.2 41.5 %all-reduce.1 = f32[32,384]{1,0:T(8,128)S(1)} all-reduce(f32[32,384]{1,0:T(8,128)S(1)} %concatenate.24), channel_id=4, replica_groups=mesh['dp'=2,'ctx'=16] {'dp','ctx'}, use_global_device_ids=true, to_apply=%region_19.20.clone | all-reduce | flops 12288 | bytes 98304
  479.0 5.2 all-to-all-start.4
  484.9 1.0 fusion.30
  486.4 1.1 copy.120
  487.5 7.2 %all-to-all-done.4 = bf16[16,32,256]{2,1,0:T(8,128)(2,1)S(1)} async-done(((bf16[16,32,256]{2,1,0:T(8,128)(2,1)}), bf16[16,32,256]{2,1,0:T(8,128)(2,1)S(1)}, u32[]{:S(2)}, u32[]{:S(2)}) %all-to-all-start.4) | async-done | bytes 262176 | tf_op jit(solution)/shard_map/all_to_all | solution.py:391
  496.3 1.0 reshape.284
  497.3 35.5 %reduce-scatter.7.cloned.1.call-done = bf16[32,1024]{1,0:T(8,128)(2,1)} async-done(((bf16[1024,1024]{1,0:T(8,128)(2,1)}), bf16[32,1024]{1,0:T(8,128)(2,1)}) %reduce-scatter.7.cloned.1.call-update) | async-done | bytes 65552 | tf_op jit(solution)/shard_map/reduce_scatter | solution.py:512
  532.8 1.5 convert_element_type.136
  534.3 19.1 %reduce-scatter.11.cloned.1.call-done = f32[128,1024]{1,0:T(8,128)} async-done(((f32[256,1024]{1,0:T(8,128)}), f32[128,1024]{1,0:T(8,128)}) %reduce-scatter.11.cloned.1.call-update) | async-done | bytes 524304 | tf_op jit(solution)/shard_map/reduce_scatter | solution.py:511
  (146 shorter events, 11.2 us)
Async XLA Ops:
  7.2 207.1 %all-gather.5.cloned.1.call-start = ((), (), s32[]{:S(2)}) async-start(), calls=%async_computation.10 | async-start | bytes 2162688 | tf_op jit(solution)/shard_map/all_gather | solution.py:431
  9.3 9.2 %copy-start.22 = (bf16[32]{0:T(256)(128)(2,1)S(1)}, bf16[32]{0:T(256)(128)(2,1)}, u32[]{:S(2)}) copy-start(bf16[32]{0:T(256)(128)(2,1)} %param.18) | copy-start | bytes 196
  9.3 9.2 %copy-start.23 = (bf16[32]{0:T(256)(128)(2,1)S(1)}, bf16[32]{0:T(256)(128)(2,1)}, u32[]{:S(2)}) copy-start(bf16[32]{0:T(256)(128)(2,1)} %param.19) | copy-start | bytes 196
  9.3 9.2 %copy-start.24 = (bf16[64]{0:T(256)(128)(2,1)S(1)}, bf16[64]{0:T(256)(128)(2,1)}, u32[]{:S(2)}) copy-start(bf16[64]{0:T(256)(128)(2,1)} %param.21) | copy-start | bytes 388
  9.3 9.2 %copy-start.25 = (bf16[32]{0:T(256)(128)(2,1)S(1)}, bf16[32]{0:T(256)(128)(2,1)}, u32[]{:S(2)}) copy-start(bf16[32]{0:T(256)(128)(2,1)} %param.23) | copy-start | bytes 196
  9.3 9.2 %copy-start.26 = (bf16[32]{0:T(256)(128)(2,1)S(1)}, bf16[32]{0:T(256)(128)(2,1)}, u32[]{:S(2)}) copy-start(bf16[32]{0:T(256)(128)(2,1)} %param.24) | copy-start | bytes 196
  9.3 9.2 %copy-start.27 = (bf16[32]{0:T(256)(128)(2,1)S(1)}, bf16[32]{0:T(256)(128)(2,1)}, u32[]{:S(2)}) copy-start(bf16[32]{0:T(256)(128)(2,1)} %param.25) | copy-start | bytes 196
  9.3 9.2 %copy-start.28 = (bf16[128]{0:T(256)(128)(2,1)S(1)}, bf16[128]{0:T(256)(128)(2,1)}, u32[]{:S(2)}) copy-start(bf16[128]{0:T(256)(128)(2,1)} %param.27) | copy-start | bytes 772
  9.3 9.2 %copy-start.29 = (bf16[32]{0:T(256)(128)(2,1)S(1)}, bf16[32]{0:T(256)(128)(2,1)}, u32[]{:S(2)}) copy-start(bf16[32]{0:T(256)(128)(2,1)} %param.29) | copy-start | bytes 196
  9.3 51.8 %copy-start.21 = (bf16[32,4096]{1,0:T(8,128)(2,1)S(1)}, bf16[32,4096]{1,0:T(8,128)(2,1)}, u32[]{:S(2)}) copy-start(bf16[32,4096]{1,0:T(8,128)(2,1)} %param.26) | copy-start | bytes 786436
  9.9 52.5 %copy-start.30 = (s32[1,128]{1,0:T(1,128)S(1)}, s32[1,128]{1,0:T(1,128)}, u32[]{:S(2)}) copy-start(s32[1,128]{1,0:T(1,128)} %param.17) | copy-start | bytes 1540
  11.1 109.5 %all-to-all-start = ((bf16[16,32,256]{2,1,0:T(8,128)(2,1)}), bf16[16,32,256]{2,1,0:T(8,128)(2,1)S(1)}, u32[]{:S(2)}, u32[]{:S(2)}) async-start(bf16[16,32,256]{2,1,0:T(8,128)(2,1)} %copy.95), calls=%async_computation | async-start | bytes 524288 | tf_op jit(solution)/shard_map/all_to_all | solution.py:391
  112.7 3.5 copy-start.1
  120.5 29.3 %all-to-all-start.2 = ((bf16[16,32,256]{2,1,0:T(8,128)(2,1)}), bf16[16,32,256]{2,1,0:T(8,128)(2,1)}, u32[]{:S(2)}, u32[]{:S(2)}) async-start(bf16[16,32,256]{2,1,0:T(8,128)(2,1)} %copy.99), calls=%async_computation.2 | async-start | bytes 524288 | tf_op jit(solution)/shard_map/all_to_all | solution.py:391
  133.9 0.8 copy-start.17
  145.9 1.0 copy-start
  149.8 64.4 %all-to-all-start.1 = ((bf16[16,128,64]{1,2,0:T(8,128)(2,1)}), bf16[16,128,64]{1,2,0:T(8,128)(2,1)}, u32[]{:S(2)}, u32[]{:S(2)}) async-start(bf16[16,128,64]{1,2,0:T(8,128)(2,1)} %copy.97), calls=%async_computation.1 | async-start | bytes 524288 | tf_op jit(solution)/shard_map/all_to_all | solution.py:391
  156.6 37.6 %copy-start.20 = (bf16[128,1024]{1,0:T(8,128)(2,1)S(1)}, bf16[128,1024]{1,0:T(8,128)(2,1)}, u32[]{:S(2)}) copy-start(bf16[128,1024]{1,0:T(8,128)(2,1)} %param.28) | copy-start | bytes 786436
  156.6 57.6 %copy-start.3 = (bf16[1,128,1024]{2,1,0:T(8,128)(2,1)S(1)}, bf16[1,128,1024]{2,1,0:T(8,128)(2,1)}, u32[]{:S(2)}) copy-start(bf16[1,128,1024]{2,1,0:T(8,128)(2,1)} %param.15) | copy-start | bytes 786436
  217.6 31.4 %copy-start.13 = (bf16[32,32,256]{2,1,0:T(8,128)(2,1)S(1)}, bf16[32,32,256]{2,1,0:T(8,128)(2,1)}, u32[]{:S(2)}) copy-start(bf16[32,32,256]{2,1,0:T(8,128)(2,1)} %all_gather.26) | copy-start | bytes 1572868
  249.0 3.5 copy-start.19
  252.5 3.4 copy-start.31
  255.9 33.6 %copy-start.9 = (bf16[4,2,2,128,1024]{4,3,2,1,0:T(8,128)(2,1)S(1)}, bf16[4,2,2,128,1024]{4,3,2,1,0:T(8,128)(2,1)}, u32[]{:S(2)}) copy-start(bf16[4,2,2,128,1024]{4,3,2,1,0:T(8,128)(2,1)} %line_gather4.1) | copy-start | bytes 12582916
  289.6 4.1 copy-start.14
  293.6 3.3 copy-start.11
  296.9 37.8 %copy-start.15 = (f32[128,1024]{1,0:T(8,128)S(1)}, f32[128,1024]{1,0:T(8,128)}, u32[]{:S(2)}) copy-start(f32[128,1024]{1,0:T(8,128)} %line_scatter3.1) | copy-start | bytes 1572868
  296.9 37.8 %copy-start.16 = (bf16[1,128,1024]{2,1,0:T(8,128)(2,1)S(1)}, bf16[1,128,1024]{2,1,0:T(8,128)(2,1)}, u32[]{:S(2)}) copy-start(bf16[1,128,1024]{2,1,0:T(8,128)(2,1)} %param.16) | copy-start | bytes 786436
  333.2 4.3 copy-start.4
  336.7 0.8 copy-start.5
  340.8 14.3 %all-to-all-start.3 = ((bf16[16,128,64]{1,2,0:T(8,128)(2,1)}), bf16[16,128,64]{1,2,0:T(8,128)(2,1)}, u32[]{:S(2)}, u32[]{:S(2)}) async-start(bf16[16,128,64]{1,2,0:T(8,128)(2,1)} %bitcast.162), calls=%async_computation.3 | async-start | bytes 524288 | tf_op jit(solution)/shard_map/all_to_all | solution.py:391
  345.0 87.4 %reduce-scatter.9.cloned.1.call-start = ((), (), s32[]{:S(2)}) async-start(), calls=%async_computation.13 | async-start | bytes 786432 | tf_op jit(solution)/shard_map/reduce_scatter | solution.py:504
  345.2 4.8 copy-start.10
  345.3 4.8 copy-start.12
  352.2 126.8 %reduce-scatter.5.cloned.1.call-start = ((), (), s32[]{:S(2)}) async-start(), calls=%async_computation.11 | async-start | bytes 786432 | tf_op jit(solution)/shard_map/reduce_scatter | solution.py:504
  359.0 3.5 copy-start.2
  375.1 2.2 copy-start.8
  377.3 2.5 copy-start.6
  379.8 153.0 %reduce-scatter.7.cloned.1.call-start = ((), (), s32[]{:S(2)}) async-start(), calls=%async_computation.12 | async-start | bytes 2162688 | tf_op jit(solution)/shard_map/reduce_scatter | solution.py:512
  382.8 170.6 %reduce-scatter.11.cloned.1.call-start = ((), (), s32[]{:S(2)}) async-start(), calls=%async_computation.14 | async-start | bytes 1572864 | tf_op jit(solution)/shard_map/reduce_scatter | solution.py:511
  383.6 5.4 copy-start.18
  430.3 54.5 %copy-start.7 = (f32[128,1024]{1,0:T(8,128)S(1)}, f32[128,1024]{1,0:T(8,128)}, u32[]{:S(2)}) copy-start(f32[128,1024]{1,0:T(8,128)} %line_scatter6.1) | copy-start | bytes 1572868
  432.4 46.6 %all-to-all-start.5 = ((bf16[16,32,256]{2,1,0:T(8,128)(2,1)}), bf16[16,32,256]{2,1,0:T(8,128)(2,1)S(1)}, u32[]{:S(2)}, u32[]{:S(2)}) async-start(bf16[16,32,256]{2,1,0:T(8,128)(2,1)} %bitcast.176), calls=%async_computation.8 | async-start | bytes 524288 | tf_op jit(solution)/shard_map/all_to_all | solution.py:391
  479.0 15.7 %all-to-all-start.4 = ((bf16[16,32,256]{2,1,0:T(8,128)(2,1)}), bf16[16,32,256]{2,1,0:T(8,128)(2,1)S(1)}, u32[]{:S(2)}, u32[]{:S(2)}) async-start(bf16[16,32,256]{2,1,0:T(8,128)(2,1)} %bitcast.177), calls=%async_computation.5 | async-start | bytes 524288 | tf_op jit(solution)/shard_map/all_to_all | solution.py:391
Sparse Core Ops, SparseCore 0:
  10.9 59.5 all-gather.4
  352.3 15.4 reduce-scatter.8
  379.9 12.7 reduce-scatter.4
  394.8 137.9 reduce-scatter.6
  535.6 17.8 reduce-scatter.10

commit v3 on v2

v3 whole, which is shorter than its diff:
```python
import functools
import math

import jax
import jax.numpy as jnp
from jax import lax
from jax.experimental import pallas as pl
from jax.experimental.pallas import tpu as pltpu
from jax.sharding import PartitionSpec as P

HEADS = 16
EPSILON = 1e-05
QB = 256
F32, BF16 = jnp.float32, jnp.bfloat16
NT = (((1,), (1,)), ((), ()))
TN = (((0,), (0,)), ((), ()))
MESH = pl.DeviceIdType.MESH
DMA = pltpu.SemaphoreType.DMA
VMEM_LIMIT = 60 << 20


def dot(x, y, dims=(((1,), (0,)), ((), ()))):
    return lax.dot_general(x, y, dims, preferred_element_type=F32)


def remote(src, dst, send, recv, peer):
    return pltpu.make_async_remote_copy(
        src_ref=src, dst_ref=dst, send_sem=send, recv_sem=recv, device_id=peer, device_id_type=MESH
    )


def greet(peers):
    barrier = pltpu.get_barrier_semaphore()
    for peer in peers:
        pl.semaphore_signal(barrier, inc=1, device_id=peer, device_id_type=MESH)
    pl.semaphore_wait(barrier, len(peers))


def greet_all(n_dp, n):
    barrier = pltpu.get_barrier_semaphore()
    flat = lax.axis_index("dp") * n + lax.axis_index("ctx")

    def signal(j, _):
        f = lax.rem(flat + j, n_dp * n)
        pl.semaphore_signal(barrier, inc=1, device_id={"dp": f // n, "ctx": f % n}, device_id_type=MESH)
        return 0

    lax.fori_loop(1, n_dp * n, signal, 0)
    pl.semaphore_wait(barrier, n_dp * n - 1)


class ToAll:
    def __init__(self, n_dp, n, block, into, sems, only_ctx=False):
        self.n, self.block, self.into, self.only = n, block, into, only_ctx
        self.send, self.recv = sems
        self.count = n if only_ctx else n_dp * n
        self.me = lax.axis_index("ctx") if only_ctx else lax.axis_index("dp") * n + lax.axis_index("ctx")

    def copy(self, j):
        f = lax.rem(self.me + j, self.count)
        peer = {"ctx": f} if self.only else {"dp": f // self.n, "ctx": f % self.n}
        return remote(self.block(f), self.into.at[self.me], self.send.at[j], self.recv.at[j], peer)

    def each(self, act):
        def step(j, _):
            act(self.copy(j))
            return 0

        lax.fori_loop(1, self.count, step, 0)

    def start(self):
        self.each(lambda c: c.start())

    def wait_recv(self):
        self.each(lambda c: c.wait_recv())

    def wait_send(self):
        self.each(lambda c: c.wait_send())


def own_bit(dim):
    axis, b = dim
    return lax.axis_index(axis) // (1 << b) % 2


def partner(dim):
    axis, b = dim
    return {axis: lax.axis_index(axis) + (1 - 2 * own_bit(dim)) * (1 << b)}


def cube_plan(n, rows):
    top = n.bit_length() - 2
    dims = [("dp", 0)] + [("ctx", b) for b in range(top - 1, 0, -1)] + [("ctx", 0)]
    links = len(dims) - 1
    size = -(-rows // (16 * links)) * 16
    cuts = [min(rows, size * i) for i in range(links)] + [rows]
    return dims, [(cuts[i], cuts[i + 1], [(i + j) % links for j in range(links)]) for i in range(links)], True


def all_plan(n_dp, n, rows):
    dims = [("dp", b) for b in range(n_dp.bit_length() - 2, -1, -1)] + [("ctx", b) for b in range(n.bit_length() - 2, -1, -1)]
    links = len(dims) - 1
    order = list(range(links))
    half = rows // 2
    return dims, [(0, half, order), (half, rows, order[2:] + order[:2])], False


class Pairwise:
    def __init__(self, plan, sems):
        self.dims, self.orders, self.core_first = plan
        self.links = len(self.dims) - 1
        self.link_send, self.link_recv, self.core_send, self.core_recv = sems
        self.mine = [own_bit(d) for d in self.dims]

    def index(self, links, core, tail=()):
        links = tuple(links)
        return ((core,) + links if self.core_first else links + (core,)) + tuple(tail)

    def peers(self):
        return [partner(d) for d in self.dims]


class Gather(Pairwise):
    def __init__(self, plan, buf, sems):
        super().__init__(plan, sems)
        self.buf = buf

    @staticmethod
    def sems(plan):
        links, parts = len(plan[0]) - 1, len(plan[1])
        return [DMA((parts, links))] * 2 + [DMA((parts * links + 1,))] * 2

    def own(self):
        return self.index(self.mine[:-1], self.mine[-1])

    def region(self, part, done, flip=None):
        lo, hi, _ = self.orders[part]
        where = [slice(None) if i in done else (1 - m if i == flip else m) for i, m in enumerate(self.mine[:-1])]
        return self.index(where, self.mine[-1], (pl.ds(lo, hi - lo),))

    def copy(self, where, send, recv, dim):
        return remote(self.buf.at[where], self.buf.at[where], send, recv, partner(self.dims[dim]))

    def link(self, part, k):
        order = self.orders[part][2]
        return self.copy(self.region(part, order[:k]), self.link_send.at[part, k], self.link_recv.at[part, k], order[k])

    def core(self, part, k):
        order = self.orders[part][2]
        at = part * self.links + k + 1
        return self.copy(self.region(part, order[:k], order[k]), self.core_send.at[at], self.core_recv.at[at], self.links)

    def core_own(self):
        return self.copy(self.own(), self.core_send.at[0], self.core_recv.at[0], self.links)

    def start(self):
        for part in range(len(self.orders)):
            self.link(part, 0).start()
        self.core_own().start()

    def step(self, k):
        for part in range(len(self.orders)):
            self.link(part, k).wait_recv()
            if k + 1 < self.links:
                self.link(part, k + 1).start()
            self.core(part, k).start()

    def core_wait(self):
        self.core_own().wait_recv()
        for part in range(len(self.orders)):
            for k in range(self.links):
                self.core(part, k).wait_recv()

    def finish(self):
        self.core_own().wait_send()
        for part in range(len(self.orders)):
            for k in range(self.links):
                self.link(part, k).wait_send()
                self.core(part, k).wait_send()


class Scatter(Pairwise):
    def __init__(self, plan, terms, bufs, sems):
        super().__init__(plan, sems)
        self.terms, self.run, self.bufs = terms, bufs[0], bufs[1:]

    @staticmethod
    def sems(plan):
        links, parts = len(plan[0]) - 1, len(plan[1])
        return [DMA((parts, links))] * 2 + [DMA((2,))] * 2

    @staticmethod
    def scratch(plan, rows, cols):
        links = len(plan[0]) - 1
        return [pltpu.VMEM((2,) * links + (rows, cols), BF16)] + [
            pltpu.VMEM((2,) * (links - 1 - k) + (rows, cols), BF16) for k in range(links)
        ]

    def core(self, half):
        where = (half,) + (slice(None),) * (self.links - 1)
        return remote(
            self.terms.at[self.index(where, 1 - self.mine[-1])], self.run.at[where],
            self.core_send.at[half], self.core_recv.at[half], partner(self.dims[-1]),
        )

    def where(self, part, k, flip):
        lo, hi, order = self.orders[part]
        order = order[::-1]
        d, gone = order[k], order[:k]
        at = []
        for i in range(self.links):
            if i == d:
                at.append(1 - self.mine[i] if flip else self.mine[i])
            else:
                at.append(self.mine[i] if i in gone else slice(None))
        return at, d, (pl.ds(lo, hi - lo),)

    def link(self, part, k):
        at, d, tail = self.where(part, k, True)
        return remote(
            self.run.at[tuple(at) + tail], self.bufs[k].at[(slice(None),) * (self.links - 1 - k) + tail],
            self.link_send.at[part, k], self.link_recv.at[part, k], partner(self.dims[d]),
        )

    def add_core(self, half):
        self.core(half).wait_recv()
        inner = self.links - 1
        for i in range(1 << inner):
            at = (half,) + tuple((i >> (inner - 1 - j)) & 1 for j in range(inner))
            own = self.terms[self.index(at, self.mine[-1])]
            self.run[at] = (self.run[at].astype(F32) + own.astype(F32)).astype(BF16)

    def start_links(self):
        for part in range(len(self.orders)):
            self.link(part, 0).start()

    def step(self, k, out=None):
        for part in range(len(self.orders)):
            at, _, tail = self.where(part, k, False)
            self.link(part, k).wait_recv()
            free = self.links - 1 - k
            for i in range(1 << free):
                idx = [(i >> (free - 1 - j)) & 1 for j in range(free)]
                rest = iter(idx)
                to = tuple(next(rest) if isinstance(v, slice) else v for v in at) + tail
                total = self.run[to].astype(F32) + self.bufs[k][tuple(idx) + tail].astype(F32)
                if k + 1 < self.links:
                    self.run[to] = total.astype(BF16)
                else:
                    out[tail[0], :] = total
            if k + 1 < self.links:
                self.link(part, k + 1).start()

    def finish(self):
        for half in range(2):
            self.core(half).wait_send()
        for part in range(len(self.orders)):
            for k in range(self.links):
                self.link(part, k).wait_send()


class Line:
    def __init__(self, n):
        self.n, self.ys = n, n // 8
        me = lax.axis_index("ctx")
        self.z, self.y, self.c = me // (2 * self.ys), me // 2 % self.ys, me % 2
        high = self.z // 2
        self.slots = [3 - 3 * high, 2 - high, self.z + 1 - 2 * (self.z % 2), self.z]
        self.inner = (self.z == 1) | (self.z == 2)
        self.outer = (self.z == 0) | (self.z == 3)
        self.side = (self.z + 1) // 2 % 2
        self.near = self.at(self.slots[2], self.y, self.c)
        self.far = self.at(self.z + 1 - 2 * high, self.y, self.c)
        self.core = self.at(self.z, self.y, 1 - self.c)

    def at(self, z, y, c):
        return {"ctx": (z * self.ys + y) * 2 + c}

    def others(self):
        return [(self.y + d) % self.ys for d in range(1, self.ys)]


class LineGather:
    def __init__(self, line, buf, sems):
        self.l, self.buf = line, buf
        self.zs, self.zr, self.ys, self.yr, self.ks, self.kr = sems

    @staticmethod
    def sems(n):
        ys = n // 8
        return [DMA((5,)), DMA((3,)), DMA((ys - 1, 4)), DMA((ys - 1, 4)), DMA((ys, 4)), DMA((ys, 4))]

    def move(self, z, y, c, send, recv, peer):
        ref = self.buf.at[z, y, c]
        return remote(ref, ref, send, recv, peer)

    def zcopy(self, i):
        l = self.l
        slot, peer, into = [(3, l.near, 0), (3, l.far, 1), (2, l.far, 2), (1, l.near, 1), (0, l.near, 2)][i]
        return self.move(l.slots[slot], l.y, l.c, self.zs.at[i], self.zr.at[into], peer)

    def ycopy(self, d, slot):
        l = self.l
        return self.move(l.slots[slot], l.y, l.c, self.ys.at[d, slot], self.yr.at[d, slot], l.at(l.z, l.others()[d], l.c))

    def kcopy(self, d, slot):
        l = self.l
        y = l.y if d == 0 else (l.y + l.ys - d) % l.ys
        return self.move(l.slots[slot], y, l.c, self.ks.at[d, slot], self.kr.at[d, slot], l.core)

    def spread(self, slot):
        for d in range(self.l.ys - 1):
            self.ycopy(d, slot).start()
        self.kcopy(0, slot).start()

    def start(self):
        self.zcopy(0).start()

        @pl.when(self.l.inner)
        def _():
            self.zcopy(1).start()

        self.spread(3)

    def z_step(self, r):
        self.zcopy((0, 3, 4)[r]).wait_recv()

        @pl.when(self.l.inner)
        def _():
            self.zcopy(2 + r).start()

        self.spread(2 - r)

    def y_step(self, slot):
        for d in range(self.l.ys - 1):
            self.ycopy(d, slot).wait_recv()
            self.kcopy(d + 1, slot).start()

    def run(self):
        self.start()
        for r in range(3):
            self.z_step(r)
            self.y_step(3 - r)
        self.y_step(0)

    def core_wait(self, slot):
        for d in range(self.l.ys):
            self.kcopy(d, slot).wait_recv()

    def finish(self):
        self.zcopy(0).wait_send()

        @pl.when(self.l.inner)
        def _():
            for i in range(1, 5):
                self.zcopy(i).wait_send()

        for slot in range(4):
            for d in range(self.l.ys - 1):
                self.ycopy(d, slot).wait_send()
            for d in range(self.l.ys):
                self.kcopy(d, slot).wait_send()


class LineScatter:
    def __init__(self, line, acc, kbuf, ybuf, zbuf, sems):
        self.l, self.acc, self.kbuf, self.ybuf, self.zbuf = line, acc, kbuf, ybuf, zbuf
        self.zs, self.zr, self.ys, self.yr, self.ks, self.kr = sems

    @staticmethod
    def sems(n):
        ys = n // 8
        return [DMA((3,)), DMA((2, 3)), DMA((ys - 1, 4)), DMA((ys - 1, 4)), DMA((ys, 4)), DMA((ys, 4))]

    @staticmethod
    def scratch(n, rows, cols):
        ys = n // 8
        return [pltpu.VMEM((4, ys, rows, cols), BF16), pltpu.VMEM((ys - 1, 4, rows, cols), BF16), pltpu.VMEM((2, 3, rows, cols), BF16)]

    def y_of(self, d):
        return self.l.y if d == 0 else self.l.others()[d - 1]

    def kcopy(self, d, slot):
        l = self.l
        z, y = l.slots[slot], self.y_of(d)
        return remote(self.acc.at[z, y, 1 - l.c], self.kbuf.at[z, y], self.ks.at[d, slot], self.kr.at[d, slot], l.core)

    def ycopy(self, d, slot):
        l = self.l
        z, y = l.slots[slot], self.y_of(d + 1)
        return remote(self.acc.at[z, y, l.c], self.ybuf.at[d, slot], self.ys.at[d, slot], self.yr.at[d, slot], l.at(l.z, y, l.c))

    def zcopy(self, slot):
        l = self.l
        return remote(self.acc.at[l.slots[slot], l.y, l.c], self.zbuf.at[l.side, slot], self.zs.at[slot], self.zr.at[l.side, slot], l.far if slot < 2 else l.near)

    def zwait(self, side, slot):
        buf = self.zbuf.at[side, slot]
        remote(buf, buf, self.zs.at[slot], self.zr.at[side, slot], self.l.near).wait_recv()
        return self.zbuf[side, slot].astype(F32)

    def own(self, slot):
        return (self.l.slots[slot], self.l.y, self.l.c)

    def core_start(self, slot):
        for d in range(self.l.ys - 1, -1, -1):
            self.kcopy(d, slot).start()

    def core_step(self, slot):
        l = self.l
        for d in list(range(1, l.ys)) + [0]:
            z, y = l.slots[slot], self.y_of(d)
            self.kcopy(d, slot).wait_recv()
            self.acc[z, y, l.c] = (self.acc[z, y, l.c].astype(F32) + self.kbuf[z, y].astype(F32)).astype(BF16)
            if d > 0:
                self.ycopy(d - 1, slot).start()

    def y_sum(self, slot):
        total = self.acc[self.own(slot)].astype(F32)
        for d in range(self.l.ys - 1):
            self.ycopy(d, slot).wait_recv()
            total = total + self.ybuf[d, slot].astype(F32)
        return total

    def z_step(self, slot):
        l, own = self.l, self.own(slot)
        total = self.y_sum(slot)
        self.acc[own] = total.astype(BF16)
        @pl.when(l.inner)
        def _():
            self.acc[own] = (self.acc[own].astype(F32) + self.zwait(*((0, slot) if slot < 2 else (1, 0)))).astype(BF16)

        self.zcopy(slot).start()

    def last(self, out):
        l = self.l
        out[...] = self.y_sum(3)

        @pl.when(l.inner)
        def _():
            out[...] += self.zwait(0, 2) + self.zwait(1, 1)

        @pl.when(l.outer)
        def _():
            out[...] += self.zwait(1, 2)

    def finish(self):
        for slot in range(4):
            for d in range(self.l.ys):
                self.kcopy(d, slot).wait_send()
            for d in range(self.l.ys - 1):
                self.ycopy(d, slot).wait_send()
        for slot in range(3):
            self.zcopy(slot).wait_send()


G1, C1, BQV, IDS, BO, G2, C2, BF, BP = range(9)


def put_ids(n, small_all, first, row, col):
    tokens = small_all.shape[2]
    for j in range(n):
        ids = small_all[first + j].astype(F32)[IDS : IDS + 1, :]
        row[:, j * tokens : (j + 1) * tokens] = ids
        col[j * tokens : (j + 1) * tokens, :] = jnp.transpose(jnp.broadcast_to(ids, (tokens, tokens)))[:, :1]


def half_row(tile_row, odd, high):
    lane = lax.broadcasted_iota(jnp.int32, tile_row.shape, 1)
    turned = pltpu.roll(tile_row, 64, 1)
    moved = jnp.where((odd == 1) == high, tile_row, turned)
    return jnp.where((lane >= 64) == high, moved, 0.0)


def normalize(rows):
    centred = rows - jnp.mean(rows, axis=-1, keepdims=True)
    rstd = lax.rsqrt(jnp.mean(centred * centred, axis=-1, keepdims=True) + EPSILON)
    return centred * rstd, rstd


def group_of(n, f):
    d, j = f // n, f % n
    return d % 2 * (n // 2) + j % (n // 2), d // 2 * 2 + j // (n // 2)


def group_peer(n, i, count):
    d, j = lax.axis_index("dp"), lax.axis_index("ctx")
    g = lax.rem(d // 2 * 2 + j // (n // 2) + i, count)
    return g, {"dp": g // 2 * 2 + d % 2, "ctx": g % 2 * (n // 2) + j % (n // 2)}


def front_kernel(n_dp, n, r, spread, cube, whole, *refs):
    refs = list(refs)
    take = lambda k: [refs.pop(0) for _ in range(k)]
    x_ref, small_ref, dy_ref = take(3)
    if spread:
        wqb, wfb, wpb, wob = take(4)
    else:
        (wq_all,) = take(1)
    small_all, first, a_ref, b_ref, o_ref, t_ref, att, dy_all = take(8)
    if spread:
        wq_all, wf_all, wp_all, wo_all = take(4)
    xbuf, prm, bqv, bias, idrow, idcol, packed, acc, tot = take(9)
    line_sems, small_sems, dy_sems, att_sems = take(6), take(2), take(4), take(2)
    if spread:
        wq_sems, wf_sems, wp_sems, wo_sems = take(2), take(2), take(2), take(4)

    tokens, width = x_ref.shape
    count = n_dp * n
    d, me = lax.axis_index("dp"), lax.axis_index("ctx")
    flat = d * n + me
    head, part = me // r, me % r
    line = Line(n)

    xg = LineGather(line, xbuf, line_sems)
    small = ToAll(n_dp, n, lambda f: small_ref, small_all, small_sems)
    dyg = Gather(cube, dy_all, dy_sems)
    xbuf[line.z, line.y, line.c] = x_ref[...]
    small_all[flat] = small_ref[...]
    dy_all[dyg.own()] = dy_ref[...]
    if spread:
        wq = ToAll(n_dp, n, lambda f: wqb.at[f % n], wq_all, wq_sems)
        wf = ToAll(n_dp, n, lambda f: wfb.at[group_of(n, f)[0]], wf_all, wf_sems)
        wog = Gather(whole, wo_all, wo_sems)
        rank, group = group_of(n, flat)
        wq_all[flat] = wqb[me]
        wf_all[flat] = wfb[rank]
        wp_all[group] = wpb[...]
        wo_all[wog.own()] = wob[...]
        wps = []
        for i in range(1, n_dp):
            _, peer = group_peer(n, i, n_dp)
            wps.append(remote(wpb, wp_all.at[group], wp_sems[0].at[i], wp_sems[1].at[i], peer))

    greet_all(n_dp, n)
    xg.start()
    small.start()
    if spread:
        wq.start()
    xg.z_step(0)
    if spread:
        for c in wps:
            c.start()
    xg.y_step(3)
    small.wait_recv()
    per = count * 128 // width
    for k in range(width // 128):
        tile = jnp.sum(small_all[k * per : (k + 1) * per].astype(F32), axis=0)
        prm[:, k * 128 : (k + 1) * 128] = tile[:8]
    per = count * 128 // (2 * width)
    for k in range(2 * width // 128):
        tile = jnp.sum(small_all[k * per : (k + 1) * per].astype(F32), axis=0)
        bqv[k : k + 1, :] = tile[BQV : BQV + 1]
    odd = head % 2
    bias[:, :128] = half_row(bqv[pl.ds(head // 2, 1), :], odd, False)
    bias[:, 128:] = half_row(bqv[pl.ds(width // 128 + head // 2, 1), :], odd, True)
    put_ids(n, small_all, d * n, idrow, idcol)
    if spread:
        wq.wait_recv()
    per_z = n // 4

    def project(slot):
        z = line.slots[slot]

        def one(i, _):
            rows = xbuf[z, i // 2, i % 2].astype(F32)
            normed, _ = normalize(rows)
            low = (normed * prm[G1 : G1 + 1, :] + prm[C1 : C1 + 1, :]).astype(BF16)
            at = pl.ds(pl.multiple_of((z * per_z + i) * tokens, tokens), tokens)
            first[at, :] = low
            return 0

        lax.fori_loop(0, per_z, one, 0)
        at = pl.ds(pl.multiple_of(z * per_z * tokens, per_z * tokens), per_z * tokens)
        qkv = (dot(first[at, :], wq_all[...].reshape(width, 256)) + bias[...]).astype(BF16)
        a_ref[at, :] = qkv[:, :128]
        b_ref[at, :] = qkv[:, 128:]

    xg.z_step(1)
    xg.y_step(2)
    xg.core_wait(3)
    project(3)
    xg.z_step(2)
    xg.y_step(1)
    xg.core_wait(2)
    project(2)
    xg.y_step(0)
    dyg.start()
    if spread:
        wf.start()
        wog.start()
    xg.core_wait(1)
    project(1)
    xg.core_wait(0)
    project(0)
    dyg.step(0)
    if spread:
        wog.step(0)

    length = b_ref.shape[0]
    kc = min(1024, length)
    half = tokens // 2
    if r > 1:
        packed[...] = jnp.zeros_like(packed)

    def per_queries(lb, _):
        gq = lb * r + part
        qs = pl.ds(pl.multiple_of(gq * QB, QB), QB)
        a = a_ref[qs, :] * 0.125
        ids = idcol[qs, :]
        acc[...] = jnp.zeros_like(acc)
        tot[...] = jnp.zeros_like(tot)

        def per_keys(kb, _):
            ks = pl.ds(pl.multiple_of(kb * kc, kc), kc)
            b = b_ref[ks, :]
            s = dot(a, b, NT)
            w = jnp.where(idrow[:, ks] <= ids, jnp.exp(s), 0.0)
            t = w[:, :128]
            for i in range(1, kc // 128):
                t = t + w[:, i * 128 : (i + 1) * 128]
            tot[...] += t
            acc[...] += dot(w.astype(BF16), b)
            return 0

        lax.fori_loop(0, jnp.minimum(((gq + 2) * QB + kc - 1) // kc, length // kc), per_keys, 0)
        t = jnp.sum(tot[...], axis=-1, keepdims=True)
        at = pl.ds(pl.multiple_of(lb * QB, QB), QB)
        t_ref[at, :] = t
        o = acc[...] / t
        o_ref[at, :] = o
        lane = lax.broadcasted_iota(jnp.int32, (half, 128), 1)
        for i in range(QB // tokens):
            lo, hi = o[i * tokens : i * tokens + half], o[i * tokens + half : (i + 1) * tokens]
            packed[gq * (QB // tokens) + i] = jnp.where(lane < 64, pltpu.roll(lo, 64, 1), hi).astype(BF16)
        return 0

    blocks = length // QB // r
    cuts = [0, blocks // 2, blocks * 3 // 4, blocks]
    for k in range(3):
        lax.fori_loop(cuts[k], cuts[k + 1], per_queries, 0)
        if k + 1 < min(3, dyg.links):
            dyg.step(k + 1)
            if spread:
                wog.step(k + 1)
    out = ToAll(n_dp, n, lambda f: packed.at[f], att, att_sems, True)
    att[me] = packed[me]
    out.start()
    for k in range(3, dyg.links):
        dyg.step(k)
    if spread:
        for k in range(3, wog.links):
            wog.step(k)
    out.wait_recv()
    dyg.core_wait()
    if spread:
        wf.wait_recv()
        for c in wps:
            c.wait_recv()
        wog.core_wait()
        for part_ in (wq, wf, wog):
            (part_.finish if part_ is wog else part_.wait_send)()
        for c in wps:
            c.wait_send()
    small.wait_send()
    out.wait_send()
    xg.finish()
    dyg.finish()


def front(n_dp, n, r, x, small, dy, weights, blocks):
    tokens, width = x.shape
    count, length = n_dp * n, n * tokens
    spread = weights is None
    cube = cube_plan(n, tokens)
    whole = all_plan(n_dp, n, 32)
    shape = jax.ShapeDtypeStruct
    outs = [
        shape((count, 16, 128), BF16), shape((length, width), BF16), shape((length, 128), BF16), shape((length, 128), BF16),
        shape((length // r, 128), F32), shape((length // r, 1), F32), shape((n, tokens // 2, 128), BF16),
        shape((2,) * len(cube[0]) + (tokens, width), BF16),
    ]
    sems = LineGather.sems(n) + [DMA((count,))] * 2 + Gather.sems(cube) + [DMA((n,))] * 2
    ins = [x, small, dy]
    if spread:
        wq, wf, wp, wo = blocks
        whole = all_plan(n_dp, n, wo.shape[0])
        outs += [
            shape((count,) + wq.shape[1:], BF16), shape((count,) + wf.shape[1:], BF16), shape((n_dp,) + wp.shape, BF16),
            shape((2,) * len(whole[0]) + wo.shape, BF16),
        ]
        sems += [DMA((count,))] * 4 + [DMA((n_dp,))] * 2 + Gather.sems(whole)
        ins += list(blocks)
    else:
        ins += [weights]
    vm = pl.BlockSpec(memory_space=pltpu.VMEM)
    return pl.pallas_call(
        functools.partial(front_kernel, n_dp, n, r, spread, cube, whole),
        out_shape=outs,
        in_specs=[vm] * len(ins),
        out_specs=[vm] * len(outs),
        scratch_shapes=[
            pltpu.VMEM((4, n // 8, 2, tokens, width), BF16), pltpu.VMEM((8, width), F32), pltpu.VMEM((2 * width // 128, 128), F32),
            pltpu.VMEM((1, 256), F32), pltpu.VMEM((1, length), F32), pltpu.VMEM((length, 1), F32),
            pltpu.VMEM((n, tokens // 2, 128), BF16), pltpu.VMEM((QB, 128), F32), pltpu.VMEM((QB, 128), F32),
        ] + sems,
        compiler_params=pltpu.CompilerParams(collective_id=1, has_side_effects=True, vmem_limit_bytes=VMEM_LIMIT),
        name="front",
    )(*ins)


def gelu_both(u):
    c = math.sqrt(2.0 / math.pi)
    t = jnp.tanh(c * (u + 0.044715 * (u * u * u)))
    half = 0.5 * (1.0 + t)
    return u * half, half + 0.5 * u * (1.0 - t * t) * (c * (1.0 + 3.0 * 0.044715 * (u * u)))


def ffn_kernel(plan, s_ref, dy_ref, wf_ref, wp_ref, bf_ref, sg_ref, out_ref, wp_grad, wf_grad, bf_grad, sbuf, grads, act, hid, acc, *rest):
    links = len(plan[0]) - 1
    bufs, rest = rest[: links + 1], rest[links + 1 :]
    g = Gather(plan, sbuf, rest[:4])
    s = Scatter(plan, acc, bufs, rest[4:])
    tokens, width = s_ref.shape
    quarter = (1 << (links - 1)) * tokens
    span = (1 << (links - 1),) + (tokens, width)
    sbuf[g.own()] = s_ref[...]
    greet(g.peers())
    g.start()
    core = g.mine[-1]

    def rows(c, a):
        return pl.ds(pl.multiple_of((2 * c + a) * quarter, quarter), quarter)

    inner = (slice(None),) * (links - 1)

    def grad_part(i):
        dy = dy_ref[(i // 2, i % 2) + inner].reshape(quarter, width)
        grads[rows(i // 2, i % 2), :] = dot(dy, wp_ref[...], NT)

    for k in range(links):
        grad_part(k)
        g.step(k)
    for k in range(links, 4):
        grad_part(k)
    g.core_wait()
    bf_grad[...] = jnp.zeros_like(bf_grad)

    def hidden_part(c, a):
        at = rows(c, a)
        low = sbuf[(c, a) + inner].reshape(quarter, width)
        active, slope = gelu_both(dot(low, wf_ref[...]) + bf_ref[...])
        act[at, :] = active.astype(BF16)
        h = (slope * grads[at, :]).astype(BF16)
        hid[at, :] = h
        bf_grad[...] += jnp.sum(h.astype(F32), axis=0, keepdims=True)
        acc[(c, a) + inner] = dot(h, wf_ref[...], NT).astype(BF16).reshape((2,) * (links - 1) + (tokens, width))

    for a in range(2):
        hidden_part(1 - core, a)
        s.core(a).start()
    for a in range(2):
        hidden_part(core, a)
        s.add_core(a)
    s.start_links()

    def weight_grads(k):
        at = slice(k * 256, (k + 1) * 256)
        low = sbuf[..., at].reshape(4 * quarter, 256)
        wf_grad[at, :] = jnp.transpose(dot(hid[...], low, TN)).astype(BF16)
        dy = dy_ref[..., at].reshape(4 * quarter, 256)
        wp_grad[:, at] = dot(act[...], dy, TN).astype(BF16)

    def out_part(i):
        at = rows(i // 2, i % 2)
        out_ref[(i // 2, i % 2) + inner] = dot(act[at, :], wp_ref[...]).astype(BF16).reshape((2,) * (links - 1) + (tokens, width))

    out_part(0)
    out_part(1)
    out_part(2)
    out_part(3)
    for k in range(links):
        s.step(k, sg_ref)
        if k < 2:
            weight_grads(2 * k)
            weight_grads(2 * k + 1)
    s.finish()
    g.finish()


def ffn(n, second_low, dy_all, wf, wp, bf):
    tokens, width = second_low.shape
    units = wf.shape[1]
    plan = cube_plan(n, tokens)
    block = (2,) * len(plan[0])
    length = n * tokens
    shape = jax.ShapeDtypeStruct
    vm = pl.BlockSpec(memory_space=pltpu.VMEM)
    return pl.pallas_call(
        functools.partial(ffn_kernel, plan),
        out_shape=[
            shape((tokens, width), F32), shape(block + (tokens, width), BF16), shape((units, width), BF16),
            shape((width, units), BF16), shape((1, units), F32),
        ],
        in_specs=[vm] * 5,
        out_specs=[vm] * 5,
        scratch_shapes=[
            pltpu.VMEM(block + (tokens, width), BF16), pltpu.VMEM((length, units), F32), pltpu.VMEM((length, units), BF16),
            pltpu.VMEM((length, units), BF16), pltpu.VMEM(block + (tokens, width), BF16),
        ] + Scatter.scratch(plan, tokens, width) + Gather.sems(plan) + Scatter.sems(plan),
        compiler_params=pltpu.CompilerParams(collective_id=2, has_side_effects=True, vmem_limit_bytes=VMEM_LIMIT),
        name="ffn",
    )(second_low, dy_all, wf, wp, bf)


def normalize_back(grad, normed, rstd):
    return rstd * (
        grad
        - jnp.mean(grad, axis=-1, keepdims=True)
        - normed * jnp.mean(grad * normed, axis=-1, keepdims=True)
    )


def back_kernel(n_dp, n, r, spread, cube, whole, *refs):
    refs = list(refs)
    take = lambda k: [refs.pop(0) for _ in range(k)]
    agb, a_ref, b_ref, o_ref, t_ref, small_all, wq_ref, first, part_out, x_ref, mg_ref, g1_ref, msgs = take(13)
    if spread:
        wfg, wpg, wog = take(3)
    out_ref, ig_ref, sums = take(3)
    if spread:
        wq_got, wf_got, wp_got, wo_own = take(4)
    else:
        (wq_sum,) = take(1)
    ag, idrow, idcol, mixed, dqacc, dkv, acc, kbuf, ybuf, zbuf, fg, got, msg, columns, column_sem = take(15)
    links = len(cube[0]) - 1
    out_bufs = take(links + 1)
    if r > 1:
        dkv_got = take(1)[0]
        pair_sems = take(2)
    ag_sems, line_sems, out_sems, msg_sems = take(2), take(6), take(4), take(2)
    if spread:
        wq_part, wq_sems, wf_sems, wp_sems = *take(1), take(2), take(2), take(2)
        wo_bufs = take(len(whole[0]))
        wo_sems = take(4)

    tokens, width = x_ref.shape
    length = b_ref.shape[0]
    count = n_dp * n
    d, me = lax.axis_index("dp"), lax.axis_index("ctx")
    flat = d * n + me
    head, part = me // r, me % r
    line = Line(n)
    kc = min(1024, length)
    half = tokens // 2

    grads = ToAll(n_dp, n, lambda f: agb.at[f], ag, ag_sems, True)
    outs = Scatter(cube, part_out, out_bufs, out_sems)
    ag[me] = agb[me]
    if spread:
        wf = ToAll(n_dp, n, lambda f: wfg.at[f], wf_got, wf_sems)
        wq = ToAll(n_dp, n, lambda f: wq_part.at[f], wq_got, wq_sems)
        wo = Scatter(whole, wog, wo_bufs, wo_sems)
        wf_got[flat] = wfg[flat]
        group = group_of(n, flat)[1]
        wp_got[group] = wpg[group]
        wps = []
        for i in range(1, n_dp):
            g, peer = group_peer(n, i, n_dp)
            wps.append(remote(wpg.at[g], wp_got.at[group], wp_sems[0].at[i], wp_sems[1].at[i], peer))
    greet_all(n_dp, n)
    grads.start()
    for h in range(2):
        outs.core(h).start()
    put_ids(n, small_all, d * n, idrow, idcol)
    dkv[...] = jnp.zeros_like(dkv)
    if r > 1:
        mixed[...] = jnp.zeros_like(mixed)
    for h in range(2):
        outs.add_core(h)
    grads.wait_recv()
    outs.start_links()
    if spread:
        for h in range(2):
            wo.core(h).start()
        for c in wps:
            c.start()

    def per_queries(lb, _):
        gq = lb * r + part
        qs = pl.ds(pl.multiple_of(gq * QB, QB), QB)
        at = pl.ds(pl.multiple_of(lb * QB, QB), QB)
        lane = lax.broadcasted_iota(jnp.int32, (half, 128), 1)
        pieces = []
        for i in range(QB // tokens):
            block = ag[gq * (QB // tokens) + i].astype(F32)
            pieces += [jnp.where(lane >= 64, pltpu.roll(block, 64, 1), 0.0), jnp.where(lane >= 64, block, 0.0)]
        grad = jnp.concatenate(pieces, axis=0)
        inverse = 1.0 / t_ref[at, :]
        upper = lax.broadcasted_iota(jnp.int32, (QB, 128), 1) >= 64
        ratio = jnp.sum(jnp.where(upper, grad * o_ref[at, :], 0.0), axis=-1, keepdims=True) * inverse
        ratio = jnp.transpose(jnp.broadcast_to(ratio, (QB, 128)))[:1, :]
        do = (grad * inverse).astype(BF16)
        a = a_ref[qs, :]
        scaled = a * 0.125
        ado = jnp.concatenate([a, do], axis=0)
        ids = idrow[:, qs]
        dqacc[...] = jnp.zeros_like(dqacc)

        def per_keys(kb, _):
            ks = pl.ds(pl.multiple_of(kb * kc, kc), kc)
            b = b_ref[ks, :]
            w = jnp.where(idcol[ks, :] <= ids, jnp.exp(dot(b, scaled, NT)), 0.0)
            g = (w * (dot(b, do, NT) - ratio)).astype(BF16)
            dkv[ks, :] += dot(jnp.concatenate([g, w.astype(BF16)], axis=1), ado)
            dqacc[...] += dot(g, b, TN)
            return 0

        lax.fori_loop(0, jnp.minimum(((gq + 2) * QB + kc - 1) // kc, length // kc), per_keys, 0)
        mixed[qs, :128] = jnp.where(upper, 0.0, dqacc[...] * 0.125).astype(BF16)
        return 0

    blocks = length // QB // r
    cuts = [0, blocks * 3 // 8, blocks * 5 // 8, blocks * 3 // 4, blocks]
    for k in range(4):
        lax.fori_loop(cuts[k], cuts[k + 1], per_queries, 0)
        if k < links:
            outs.step(k, out_ref)
        if k == 0 and spread:
            wf.start()
            for h in range(2):
                wo.add_core(h)
            wo.start_links()

    low = lax.broadcasted_iota(jnp.int32, (length, 128), 1) < 64
    total = dkv[...]
    if r > 1:
        both = remote(dkv, dkv_got, pair_sems[0], pair_sems[1], line.core)
        both.start()
        both.wait()
        total = jnp.where(part == 0, total + dkv_got[...], 0.0)
    mixed[:, 128:] = jnp.where(low, total * 0.125, total).astype(BF16)

    rs = LineScatter(line, acc, kbuf, ybuf, zbuf, line_sems)
    per_z = n // 4 * tokens

    def first_grad(slot):
        z = line.slots[slot]
        at = pl.ds(pl.multiple_of(z * per_z, per_z), per_z)
        acc[z] = dot(mixed[at, :], wq_ref[...], NT).astype(BF16).reshape(n // 8, 2, tokens, width)
        rs.core_start(slot)

    def fetch(k):
        return pltpu.make_async_copy(first.at[:, pl.ds(k * 256, 256)], columns, column_sem)

    fetch(0).start()
    first_grad(0)
    for slot in range(1, 4):
        first_grad(slot)
        rs.core_step(slot - 1)
    rs.core_step(3)
    column = jnp.sum(mixed[...].astype(F32), axis=0, keepdims=True)
    odd = head % 2
    q_row = half_row(column[:, :128], 0, False)
    q_row = jnp.where(odd == 1, pltpu.roll(q_row, 64, 1), q_row)
    v_row = half_row(column[:, 128:], 1, True)
    v_row = jnp.where(odd == 1, v_row, pltpu.roll(v_row, 64, 1))

    def wq_grad(k):
        at = slice(k * 256, (k + 1) * 256)
        fetch(k).wait()
        g = jnp.transpose(dot(mixed[...], columns[...], TN))
        if k < 3:
            fetch(k + 1).start()
        if spread:
            rows = width // count
            wq_part[256 // rows * k : 256 // rows * (k + 1)] = g.astype(BF16).reshape(256 // rows, rows, 256)
        else:
            wq_sum[at, :] = g

    for k in range(3):
        wq_grad(k)
        rs.z_step(k)
    wq_grad(3)
    if spread:
        wq_got[flat] = wq_part[flat]
        wq.start()
        for k in range(wo.links):
            wo.step(k, wo_own)
    rs.last(fg)

    x = x_ref[...].astype(F32)
    n1, rstd1 = normalize(x)
    grad = fg[...]
    gain = jnp.sum(grad * n1, axis=0, keepdims=True)
    shift = jnp.sum(grad, axis=0, keepdims=True)
    per = 128 * count // width

    for k in range(width // 128):
        rows = jnp.concatenate([gain[:, k * 128 : (k + 1) * 128], shift[:, k * 128 : (k + 1) * 128]], axis=0)

        def fill(i, _, k=k, rows=rows):
            msg[k * per + i, 0:2, :] = rows
            return 0

        lax.fori_loop(0, per, fill, 0)

    def rest(f, _):
        tile = f * 2 * width // count // 128
        bqv = jnp.where(tile == head // 2, q_row, 0.0) + jnp.where(tile == width // 128 + head // 2, v_row, 0.0)
        msg[f, 2:6, :] = msgs[f, 2:6, :]
        msg[f, 6:7, :] = bqv
        msg[f, 7:8, :] = msgs[f, 7:8, :]
        return 0

    lax.fori_loop(0, count, rest, 0)
    tell_all = ToAll(n_dp, n, lambda f: msg.at[f], got, msg_sems)
    tell_all.start()
    got[flat] = msg[flat]
    ig_ref[...] = (mg_ref[...] + normalize_back(grad * g1_ref[...], n1, rstd1)).astype(BF16)
    tell_all.wait_recv()
    sums[...] = jnp.sum(got[...], axis=0)
    tell_all.wait_send()
    if spread:
        wf.wait_recv()
        wq.wait_recv()
        for c in wps:
            c.wait()
        wf.wait_send()
        wq.wait_send()
        wo.finish()
    grads.wait_send()
    outs.finish()
    rs.finish()


def back(n_dp, n, r, agb, a, b, o, t, small_all, wq, first, part_out, x, mg, g1, msgs, grads):
    tokens, width = x.shape
    count, length = n_dp * n, n * tokens
    spread = grads is not None
    cube = cube_plan(n, tokens)
    whole = None
    shape = jax.ShapeDtypeStruct
    ins = [agb, a, b, o, t, small_all, wq, first, part_out, x, mg, g1, msgs]
    outs = [shape((tokens, width), F32), shape((tokens, width), BF16), shape((8, 128), F32)]
    scratch = [
        pltpu.VMEM((n, tokens // 2, 128), BF16), pltpu.VMEM((1, length), F32), pltpu.VMEM((length, 1), F32),
        pltpu.VMEM((length, 256), BF16), pltpu.VMEM((QB, 128), F32), pltpu.VMEM((length, 128), F32),
        pltpu.VMEM((4, n // 8, 2, tokens, width), BF16),
    ] + LineScatter.scratch(n, tokens, width) + [
        pltpu.VMEM((tokens, width), F32), pltpu.VMEM((count, 8, 128), F32), pltpu.VMEM((count, 8, 128), F32),
        pltpu.VMEM((length, 256), BF16), DMA,
    ] + Scatter.scratch(cube, tokens, width)
    if r > 1:
        scratch += [pltpu.VMEM((length, 128), F32), DMA, DMA]
    scratch += [DMA((n,))] * 2 + LineScatter.sems(n) + Scatter.sems(cube) + [DMA((count,))] * 2
    if spread:
        wfg, wpg, wog = grads
        rows = width // count
        whole = all_plan(n_dp, n, rows)
        ins += [wfg, wpg, wog]
        outs += [
            shape((count, rows, 256), BF16), shape(wfg.shape, BF16), shape(wpg.shape, BF16), shape((rows, width), F32),
        ]
        scratch += [pltpu.VMEM((count, rows, 256), BF16)] + [DMA((count,))] * 4 + [DMA((n_dp,))] * 2
        scratch += Scatter.scratch(whole, rows, width) + Scatter.sems(whole)
    else:
        outs += [shape((width, 256), F32)]
    vm = pl.BlockSpec(memory_space=pltpu.VMEM)
    return pl.pallas_call(
        functools.partial(back_kernel, n_dp, n, r, spread, cube, whole),
        out_shape=outs,
        in_specs=[pl.BlockSpec(memory_space=pl.ANY) if v is first else vm for v in ins],
        out_specs=[vm] * len(outs),
        scratch_shapes=scratch,
        compiler_params=pltpu.CompilerParams(collective_id=3, has_side_effects=True, vmem_limit_bytes=VMEM_LIMIT),
        name="back",
    )(*ins)


def place(v, flat):
    pieces = 128 // v.shape[0]
    return jnp.where(jnp.arange(128) // v.shape[0] == flat % pieces, jnp.tile(v, pieces), 0)


def local(n_dp, n, inputs, cotangent, block_ids, ln1_gain, ln1_bias, w_qkv, b_qkv, w_out, b_out, ln2_gain, ln2_bias, w_fc, b_fc, w_proj, b_proj):
    tokens, width = inputs.shape[1:]
    count = n_dp * n
    rows = w_qkv.shape[0]
    units = w_proj.shape[0]
    r = n // HEADS
    hd = width // HEADS
    d, me = lax.axis_index("dp"), lax.axis_index("ctx")
    flat = d * n + me
    head = me // r
    both = ("dp", "ctx")
    x, dy = inputs[0], cotangent[0]
    halves = (n_dp // 2, 2, 2, n // 2)

    small = [place(v, flat) for v in (ln1_gain, ln1_bias, b_qkv)] + [block_ids[0].astype(BF16)]
    small += [place(v, flat) for v in (b_out, ln2_gain, ln2_bias, b_fc, b_proj)]
    small = jnp.pad(jnp.stack(small), ((0, 16 - len(small)), (0, 0)))

    def heads_of(w):
        w = w.reshape(w.shape[0], 3, HEADS, 1, hd)
        w = jnp.stack([w[:, 0], jnp.zeros_like(w[:, 0]), w[:, 1], w[:, 2]], axis=3)
        return w.reshape(w.shape[0], HEADS, 4 * hd)

    spread = rows % 16 == 0
    if spread:
        wq = jnp.repeat(jnp.transpose(heads_of(w_qkv), (1, 0, 2)), r, axis=0)
        wf = jnp.transpose(w_fc.reshape((rows,) + halves + (units,)), (2, 4, 0, 1, 3, 5)).reshape(n, rows, n_dp * units)
        weights, blocks = None, (wq, wf, w_proj, w_out)
    else:
        full = lax.all_gather(w_qkv, both, axis=0, tiled=True)
        weights = lax.dynamic_index_in_dim(heads_of(full), head, 1, keepdims=False)
        blocks = None
        wf = lax.all_gather(w_fc, both, axis=0, tiled=True).reshape((width,) + halves + (units,))
        wf = lax.dynamic_index_in_dim(wf, d % 2, 2, keepdims=False)
        wf = lax.dynamic_index_in_dim(wf, me % (n // 2), 3, keepdims=False).reshape(width, n_dp * units)
        wp = lax.all_gather(w_proj, both, axis=0, tiled=True).reshape(halves + (units, width))
        wp = lax.dynamic_index_in_dim(wp, d % 2, 1, keepdims=False)
        wp = lax.dynamic_index_in_dim(wp, me % (n // 2), 2, keepdims=False).reshape(n_dp * units, width)
        wo = lax.all_gather(w_out, both, axis=0, tiled=True)

    got = front(n_dp, n, r, x, small, dy, weights, blocks)
    small_all, first, a, b, o, t, att, dy_all = got[:8]
    if spread:
        wq, wf, wp, wo = got[8:]
        wq, wf, wp, wo = wq.reshape(width, -1), wf.reshape(width, -1), wp.reshape(-1, width), wo.reshape(width, width)
    else:
        wq = weights

    def vector(row, size):
        tiles = small_all[:, row].astype(F32).reshape(-1, 128 // size, 128)
        return jnp.sum(tiles, axis=1).reshape(1, -1)

    g1, bo, g2, c2, bp = (vector(k, rows) for k in (G1, BO, G2, C2, BP))
    bf = vector(BF, units).reshape(halves + (units,))
    bf = lax.dynamic_index_in_dim(bf, d % 2, 1, keepdims=False)
    bf = lax.dynamic_index_in_dim(bf, me % (n // 2), 2, keepdims=False).reshape(1, -1)

    att = att.reshape(HEADS, r, tokens // 2, 2, hd)
    att = att[:, 0] if r == 1 else att.sum(axis=1)
    attended_low = jnp.transpose(att, (2, 1, 0, 3)).reshape(tokens, width)
    middle = x.astype(F32) + dot(attended_low, wo) + bo
    n2, rstd2 = normalize(middle)
    second_low = (n2 * g2 + c2).astype(BF16)

    second_grad, part_out, wp_grad, wf_grad, bf_grad = ffn(n, second_low, dy_all, wf, wp, bf)

    dy = dy.astype(F32)
    middle_grad = dy + normalize_back(second_grad * g2, n2, rstd2)
    branch_low = middle_grad.astype(BF16)
    wo_grad = dot(attended_low, branch_low, TN).astype(BF16)
    agb = dot(branch_low, wo, NT).astype(BF16).reshape(2, tokens // 2, HEADS, hd)
    agb = jnp.transpose(agb, (2, 1, 0, 3)).reshape(HEADS, tokens // 2, 2 * hd)
    agb = jnp.repeat(agb, r, axis=0)

    bf_full = bf_grad.reshape(n_dp // 2, 1, 2, 1, units)
    hot = (jnp.arange(2) == d % 2).reshape(1, 2, 1, 1, 1) & (jnp.arange(n // 2) == me % (n // 2)).reshape(1, 1, 1, -1, 1)
    lines = [jnp.sum(v, axis=0).reshape(count, -1) for v in (branch_low.astype(F32), second_grad * n2, second_grad, dy)]
    lines.append(jnp.where(hot, bf_full, 0.0).reshape(count, units))
    lines = [jnp.pad(v, ((0, 0), (0, 128 - v.shape[1]))) for v in lines]
    nothing = jnp.zeros((count, 128), F32)
    msgs = jnp.stack([nothing, nothing] + lines[:4] + [nothing, lines[4]], axis=1)

    if spread:
        whole = (2,) * (count.bit_length() - 1) + (rows, width)
        grads = (wf_grad.reshape(count, rows, -1), wp_grad.reshape(n_dp, units, width), wo_grad.reshape(whole))
    else:
        grads = None
    got = back(n_dp, n, r, agb, a, b, o, t, small_all, wq, first, part_out, x, middle_grad, g1, msgs, grads)
    out_sum, input_grad, sums = got[:3]
    output = (middle + out_sum + bp).astype(BF16)
    if spread:
        wq_own, wf_own, wp_own, wo_own = got[3:]
        wq_own = jnp.sum(wq_own.astype(F32).reshape(n_dp, HEADS, r, rows, 4, hd), axis=(0, 2))
        wq_own = jnp.stack([wq_own[:, :, 0], wq_own[:, :, 2], wq_own[:, :, 3]], axis=1)
        wq_own = jnp.transpose(wq_own, (2, 1, 0, 3)).reshape(rows, 3 * width)
        wf_own = jnp.sum(wf_own.astype(F32).reshape(halves + (rows, n_dp // 2, 2, units)), axis=(0, 2))
        wf_own = jnp.transpose(wf_own, (2, 3, 0, 4, 1, 5)).reshape(rows, -1)
        wp_own = jnp.sum(wp_own.astype(F32), axis=0)
    else:
        owned = lambda v: lax.psum_scatter(v, both, scatter_dimension=0, tiled=True)
        g = got[3].reshape(width, 4, 1, hd)
        g = jnp.stack([g[:, 0], g[:, 2], g[:, 3]], axis=1)
        wq_own = owned(jnp.where((jnp.arange(HEADS) == head).reshape(1, 1, -1, 1), g, 0.0).reshape(width, 3 * width))
        g = wf_grad.astype(F32).reshape(width, n_dp // 2, 1, 2, 1, units)
        wf_own = owned(jnp.where(hot[None], g, 0.0).reshape(width, -1))
        g = wp_grad.astype(F32).reshape(n_dp // 2, 1, 2, 1, units, width)
        wp_own = owned(jnp.where(hot[..., None], g, 0.0).reshape(-1, width))
        wo_own = owned(wo_grad.astype(F32))

    def cut(row, size):
        return lax.dynamic_slice(sums[row], (flat * size % 128,), (size,))

    g1g, c1g, bqvg = cut(0, rows), cut(1, rows), cut(6, 2 * rows)
    bog, g2g, c2g, bpg = (sums[k, :rows] for k in range(2, 6))
    bfg = sums[7, :units]
    return (
        output[None], input_grad[None], g1g, c1g, wq_own, bqvg, wo_own, bog, g2g, c2g, wf_own, bfg, wp_own, bpg,
    )


def solution(mesh):
    both = ("dp", "ctx")
    act, vec, mat = P("dp", "ctx", None), P(both), P(both, None)
    return jax.shard_map(
        functools.partial(local, mesh.shape["dp"], mesh.shape["ctx"]),
        mesh=mesh,
        in_specs=(act, act, P("dp", "ctx"), vec, vec, mat, vec, mat, vec, vec, vec, mat, vec, mat, vec),
        out_specs=(act, act, vec, vec, mat, vec, mat, vec, vec, vec, mat, vec, mat, vec),
        check_vma=False,
    )
```

time: 569 us -> 336 us (0.59)
  blocking collectives: 130 us -> 0 us
  waiting for transfers between devices: 65.4 us -> 0 us
  Pallas kernels: 228 us -> 284 us
  matrix products: 37.5 us -> 3.51 us
  starting transfers between devices: 30.8 us -> 0 us
  other arithmetic: 26.3 us -> 11.5 us
  between operations: 15 us -> 1.52 us
    all_gather x5 -> x0, blocking collectives: 88.6 us -> none  [the longest x1 42.2 us: local(): small = lax.all_gather(small, ('dp', 'ctx'), axis=0).astype(F32)]
    pallas_call x8 -> x3, Pallas kernels: 228 us -> 284 us  [the longest x1 115 us: front(): pl.pallas_call(functools.partial(front_kernel, n_dp, n, r, spread, cube,...]
    reduce_scatter x4 -> x0, waiting for transfers between devices: 54.6 us -> none  [the longest x1 35.5 us: local(): lax.psum_scatter(wo_grad.astype(BF16), ('dp', 'ctx'), scatter_dimension=0...]
    unnamed x1 -> x0, blocking collectives: 41.5 us -> none
    dot_general x12 -> x3, matrix products: 37.5 us -> 3.51 us  [dot(): return lax.dot_general(x, y, dims, preferred_element_type=F32)]
    all_to_all x6 -> x0, starting transfers between devices: 30.4 us -> none  [exchange_ctx(): return lax.all_to_all(v, 'ctx', 0, 0, tiled=True)]
    all_to_all x6 -> x0, waiting for transfers between devices: 10 us -> none  [exchange_ctx(): return lax.all_to_all(v, 'ctx', 0, 0, tiled=True)]
    another operation x6 -> x24, local copies, waits for them, and re-layouts: 0.92 us -> 10.1 us  [the longest x14 5.22 us: place(): jnp.tile(v, pieces)]
  transfers between devices with their start and end apart: 11 -> 0, of which waited for: 4 -> 0; matrix products, arithmetic and copies ran while one was open for 11% -> 0% of each run, Pallas kernels for 23% -> 0%
where the time goes in v3:
time: 336 us; the launch traced here: 331 us
  Pallas kernels  284 us (85%)
  local copies, waits for them, and re-layouts  29.7 us (9%)
  other arithmetic  11.5 us (3%)
  matrix products  3.51 us (1%)
    pallas_call x1, Pallas kernels, front(): pl.pallas_call(functools.partial(front_kernel, n_dp, n, r, spread, cube,...  115 us
    pallas_call x1, Pallas kernels, back(): pl.pallas_call(functools.partial(back_kernel, n_dp, n, r, spread, cube, w...  114 us
    pallas_call x1, Pallas kernels, ffn(): pl.pallas_call(functools.partial(ffn_kernel, plan), out_shape=[shape((tok...  55.2 us

profile of v3, /device:TPU:0, one launch (start us, length us, event | category | flops | bytes accessed | tf_op | source)
XLA Modules:
  0.0 330.6 jit_solution(11964286423974234135)
XLA Ops:
  0.7 0.7 tile.75
  1.3 0.1 tile.76
  1.4 0.7 tile.32
  2.1 0.1 tile.33
  2.2 0.7 tile.71
  2.8 0.1 tile.72
  2.9 0.7 tile.73
  3.6 0.1 tile.74
  3.7 0.7 tile.30
  4.3 0.1 tile.31
  4.4 0.7 tile.34
  5.1 0.1 tile.70
  5.2 0.7 tile.28
  5.8 0.1 tile.29
  5.9 0.7 convert_element_type.107
  6.6 0.7 fusion.6
  7.3 0.6 pad.17.refs_1_
  7.9 1.2 reshape.399
  9.2 0.1 pad.26.clone
  9.3 0.1 pad_maximum_fusion
  9.4 0.4 copy.58
  9.8 1.0 reshape.400
  10.9 0.2 copy.76
  11.2 0.9 reshape.402.refs_4_
  12.1 115.4 %front.1 = (bf16[32,16,128]{2,1,0:T(8,128)(2,1)}, bf16[2048,1024]{1,0:T(8,128)(2,1)}, bf16[2048,128]{1,0:T(8,128)(2,1)}, bf16[2048,128]{1,0:T(8,128)(2,1)}, f32[...) custom-call(bf16[128,1024]{1,0:T(8,128)(2,1)} %bitcast.107, ...), custom_call_target="tpu_custom_call" | custom-call | tf_op jit(solution)/shard_map/front/pallas_call | solution.py:697
  127.4 1.3 squeeze_reshape.3
  128.8 1.1 copy.75
  129.9 1.4 reshape.403
  131.4 0.7 slice_convert_fusion
  132.1 0.5 fusion.10
  132.7 0.2 multiply_reduce_fusion.2
  132.9 0.9 add_convert_fusion.1.s_ref
  133.8 0.6 dynamic-slice_bitcast_fusion.bf_ref
  134.4 55.2 %ffn.1 = (f32[128,1024]{1,0:T(8,128)}, bf16[2,2,2,2,128,1024]{5,4,3,2,1,0:T(8,128)(2,1)}, bf16[256,1024]{1,0:T(8,128)(2,1)}, bf16[1024,256]{1,0:T(8,128)(2,1)}, f32[1,256]{1,0:T(1,128)}) custom-call(bf16[128,1024]{1,0:T(8,128)(2,1)} %add_convert_fusion.1.s_ref, bf16[2,2,2,2,128,1024]{5,4,3,2,1,0:T(8,128)(2,1)} %get-tuple-element.41.dy_ref, ...), custom_call_target="tpu_custom_call" | custom-call | tf_op jit(solution)/shard_map/ffn/pallas_call | solution.py:799
  189.6 1.3 multiply_reduce_fusion
  190.9 1.3 convert_reduce_fusion.2
  192.3 2.1 convolution_convert_fusion
  194.7 0.1 broadcast_in_dim.52
  194.8 0.1 broadcast_select_fusion
  195.1 0.8 stack.47.refs_12_
  195.9 0.8 convolution_convert_fusion.1
  196.8 0.3 reshape.408
  197.1 0.5 copy.74
  197.7 1.0 reshape_broadcast_in_dim_reshape.3.refs_0_
  198.6 0.6 reduce_sum.157
  199.2 113.7 %back.1 = (f32[128,1024]{1,0:T(8,128)}, bf16[128,1024]{1,0:T(8,128)(2,1)}, f32[8,128]{1,0:T(8,128)}, bf16[32,32,256]{2,1,0:T(8,128)(2,1)}, bf16[32,32,256]{2,1,0...) custom-call(bf16[16,64,128]{2,1,0:T(8,128)(2,1)} %reshape_broadcast_in_dim_reshape.3.refs_0_, ...), custom_call_target="tpu_custom_call" | custom-call | tf_op jit(solution)/shard_map/back/pallas_call | solution.py:1070
  313.0 2.0 reshape.431
  315.0 2.1 reduce_sum.163
  317.1 3.0 fusion.9
  320.2 0.5 copy.65
  320.6 1.0 reshape.420
  321.6 0.5 reshape.433
  322.2 0.9 reduce_sum.164
  323.1 0.3 copy.66
  323.4 0.9 reshape.423
  324.3 0.9 convert_reduce_fusion
  325.2 0.5 slice_bitcast_fusion.4
  325.7 0.6 fusion.3
  326.3 0.6 fusion.4
  326.9 0.6 fusion.5
  327.5 0.8 fusion.1
  328.3 0.5 slice_bitcast_fusion.3
  328.8 0.7 copy.79
  329.5 0.7 copy.80
  (63 shorter events, 0.8 us)
Async XLA Ops:
  3.6 7.3 %copy-start.10 = (bf16[32,4096]{1,0:T(8,128)(2,1)S(1)}, bf16[32,4096]{1,0:T(8,128)(2,1)}, u32[]{:S(2)}) copy-start(bf16[32,4096]{1,0:T(8,128)(2,1)} %param.26) | copy-start | bytes 786436
  12.0 120.0 %copy-start.2 = (bf16[1,128,1024]{2,1,0:T(8,128)(2,1)S(1)}, bf16[1,128,1024]{2,1,0:T(8,128)(2,1)}, u32[]{:S(2)}) copy-start(bf16[1,128,1024]{2,1,0:T(8,128)(2,1)} %param.15) | copy-start | bytes 786436
  127.4 4.0 %copy-start.9 = (bf16[32,16,128]{2,1,0:T(8,128)(2,1)S(1)}, bf16[32,16,128]{2,1,0:T(8,128)(2,1)}, u32[]{:S(2)}) copy-start(bf16[32,16,128]{2,1,0:T(8,128)(2,1)} %get-tuple-element.40.refs_5_) | copy-start | bytes 393220
  127.4 4.7 %copy-start = (bf16[2,2,2,2,2,32,1024]{6,5,4,3,2,1,0:T(8,128)(2,1)S(1)}, bf16[2,2,2,2,2,32,1024]{6,5,4,3,2,1,0:T(8,128)(2,1)}, u32[]{:S(2)}) copy-start(bf16[2,2,2,2,2,32,1024]{6,5,4,3,2,1,0:T(8,128)(2,1)} %get-tuple-element.39) | copy-start | bytes 6291460
  131.4 2.4 copy-start.3
  134.4 56.6 %copy-start.5 = (bf16[1,128,1024]{2,1,0:T(8,128)(2,1)S(1)}, bf16[1,128,1024]{2,1,0:T(8,128)(2,1)}, u32[]{:S(2)}) copy-start(bf16[1,128,1024]{2,1,0:T(8,128)(2,1)} %param.16) | copy-start | bytes 786436
  189.5 2.7 copy-start.4
  190.9 3.7 %copy-start.15 = (f32[1,256]{1,0:T(1,128)S(1)}, f32[1,256]{1,0:T(1,128)}, u32[]{:S(2)}) copy-start(f32[1,256]{1,0:T(1,128)} %get-tuple-element.52) | copy-start | bytes 3076
  192.3 4.5 %copy-start.1 = (f32[128,1024]{1,0:T(8,128)}, f32[128,1024]{1,0:T(8,128)S(1)}, u32[]{:S(2)}) copy-start(f32[128,1024]{1,0:T(8,128)S(1)} %get-tuple-element.67.refs_10_) | copy-start | bytes 1572868
  195.9 2.7 copy-start.13
  320.1 1.6 copy-start.6
  322.1 2.2 copy-start.8
  322.2 3.1 copy-start.14
  322.2 5.3 %copy-start.7 = (f32[128,1024]{1,0:T(8,128)S(1)}, f32[128,1024]{1,0:T(8,128)}, u32[]{:S(2)}) copy-start(f32[128,1024]{1,0:T(8,128)} %get-tuple-element.55) | copy-start | bytes 1572868
  323.1 5.7 %copy-start.11 = (bf16[128,1024]{1,0:T(8,128)(2,1)S(1)}, bf16[128,1024]{1,0:T(8,128)(2,1)}, u32[]{:S(2)}) copy-start(bf16[128,1024]{1,0:T(8,128)(2,1)} %get-tuple-element.56) | copy-start | bytes 786436
  323.4 6.1 %copy-start.12 = (f32[32,1024]{1,0:T(8,128)S(1)}, f32[32,1024]{1,0:T(8,128)}, u32[]{:S(2)}) copy-start(f32[32,1024]{1,0:T(8,128)} %get-tuple-element.117) | copy-start | bytes 393220
